TPU v7x, 32 devices: a whole 2x2x4 slice. The times are simulated.
32 devices in a mesh: blk: 8 (over y, x, core), head: 4 (over z).
Axes of the slice: x: 2, y: 2, z: 4, core: 2. Of those that a mesh axis runs over, the one named last changes fastest.
Arguments:
- queries: float32 [16, 2048, 128], P('head', 'blk'), may hold values from -6 to 6
- key_rows: float32 [16, 2048, 128], P('head', 'blk'), may hold values from -1 to 1
- value_rows: float32 [16, 2048, 128], P('head', 'blk'), may hold values from -6 to 6
- memory_keys: bfloat16 [16, 16384, 128], P('head', 'blk'), may hold values from -1 to 1
- memory_values: bfloat16 [16, 16384, 128], P('head', 'blk'), may hold values from -6 to 6
- gate_bias: float32 [16], P('head'), may hold values from -2 to 2
- norm_gain: float32 [16, 128], P('head'), may hold values from 0.1 to 1.9
- block_ids: int32 [16, 16], P('blk'), may hold values from 0 to 127, as said below
- drop_seed: int32 [1], replicated, may hold values from 0 to 999999
- out_grad: float32 [16, 2048, 128], P('head', 'blk'), may hold values from -4 to 4
Outputs:
- query_grad: float32 [16, 2048, 128], P('head', 'blk')
- key_grad: float32 [16, 2048, 128], P('head', 'blk')
- value_grad: float32 [16, 2048, 128], P('head', 'blk')
- memory_key_grad: float32 [16, 16384, 128], P('head', 'blk')
- memory_value_grad: float32 [16, 16384, 128], P('head', 'blk')
Inputs may be any that keep to these rules, and one draw needn't show every extreme that they name: `block_ids`: memory block m is held by the device of blk index m // 16. Among the 32 ids of the query blocks of one device, at most 5 (counted with repeats) and at most 5 distinct ones are held by any one device.
All inputs are finite; a program needn't handle non-finite values.
Results may differ from a plain program's by a relative error of at most 0.0004.
Values may be sent and summed in bfloat16 or wider, within the bound.
A program may use at most 128 MiB of HBM per device.

v0:
```python
import math

import jax
import jax.numpy as jnp
from jax import lax
from jax.sharding import PartitionSpec as P

H = 16
TB = 128
R = 16


highest = lax.Precision.HIGHEST
drop_level = 103
norm_eps = 1e-06


def from_behind(x, axis, by):
    devices = lax.axis_size(axis)
    pairs = [(i, i + by) for i in range(devices) if 0 <= i + by < devices]
    return lax.ppermute(x, axis, pairs)


def mix_bits(counter, seed_value):
    state = counter * jnp.int32(-1640531535) + seed_value
    state = state ^ lax.shift_right_logical(state, jnp.int32(15))
    state = state * jnp.int32(739982445)
    state = state ^ lax.shift_right_logical(state, jnp.int32(12))
    state = state * jnp.int32(695872825)
    state = state ^ lax.shift_right_logical(state, jnp.int32(15))
    return jnp.where(state & 1023 >= drop_level, 1.0 / 0.9, 0.0)


def local(
    queries,
    key_rows,
    value_rows,
    memory_keys,
    memory_values,
    gate_bias,
    norm_gain,
    block_ids,
    drop_seed,
    out_grad,
):
    heads_dev, shard_rows, head_width = queries.shape
    block_count = shard_rows // TB
    score_scale = 1.0 / math.sqrt(head_width)
    blk_count = lax.axis_size("blk")
    blk_index = lax.axis_index("blk")
    gate_mix = jax.nn.sigmoid(gate_bias)[:, None, None]
    prev_keys, prev_values = from_behind((key_rows, value_rows), "blk", 1)
    near_keys = jnp.concatenate([prev_keys, key_rows], 1)
    near_values = jnp.concatenate([prev_values, value_rows], 1)
    row_pos = jnp.arange(shard_rows, dtype=jnp.int32)[:, None]
    col_pos = jnp.arange(2 * shard_rows, dtype=jnp.int32)[None, :]
    in_window = (
        (col_pos > row_pos)
        & (col_pos <= row_pos + shard_rows)
        & (blk_index * shard_rows - shard_rows + col_pos >= 0)
    )
    near_scores = jnp.einsum("hqd,hkd->hqk", queries, near_keys, precision=highest) * score_scale
    near_exp = jnp.where(in_window[None], jnp.exp(near_scores), 0.0)
    near_total = jnp.sum(near_exp, -1, keepdims=True)
    near_weights = near_exp / near_total
    local_out = jnp.einsum("hqk,hkd->hqd", near_weights, near_values, precision=highest)
    slot_count = block_count * R
    flat_ids = block_ids.reshape(-1)
    mb_dev = memory_keys.shape[1] // TB
    owners = flat_ids // mb_dev
    local_ids = flat_ids % mb_dev
    position = jnp.arange(slot_count, dtype=jnp.int32)
    earlier = position[None, :] < position[:, None]
    same_owner = owners[:, None] == owners[None, :]
    spread = (block_count * (R - 1) + blk_count - 2) // (blk_count - 1)
    capacity = max(block_count, spread)
    writer = jnp.ones((slot_count,), bool)
    rank = jnp.sum((earlier & same_owner).astype(jnp.int32), axis=1)
    slot_of = owners * capacity + rank
    buffer_size = blk_count * capacity
    targets = jnp.arange(buffer_size, dtype=jnp.int32)[:, None] == slot_of[None, :]
    wanted = jnp.sum(jnp.where(targets & writer[None, :], local_ids[None, :], 0), axis=1)
    asked = lax.all_to_all(wanted, "blk", split_axis=0, concat_axis=0, tiled=True)
    key_store = memory_keys.reshape(heads_dev, mb_dev, TB, head_width)
    value_store = memory_values.reshape(heads_dev, mb_dev, TB, head_width)
    sent_keys = jnp.take(key_store, asked, axis=1)
    sent_values = jnp.take(value_store, asked, axis=1)
    got_keys, got_values = (
        lax.all_to_all(sent_keys, "blk", split_axis=1, concat_axis=1, tiled=True),
        lax.all_to_all(sent_values, "blk", split_axis=1, concat_axis=1, tiled=True),
    )
    far_keys = (
        jnp.take(got_keys, slot_of, axis=1)
        .astype(jnp.float32)
        .reshape(heads_dev, block_count, R * TB, head_width)
    )
    far_values = (
        jnp.take(got_values, slot_of, axis=1)
        .astype(jnp.float32)
        .reshape(heads_dev, block_count, R * TB, head_width)
    )
    query_blocks = queries.reshape(heads_dev, block_count, TB, head_width)
    far_scores = (
        jnp.einsum("hbqd,hbkd->hbqk", query_blocks, far_keys, precision=highest) * score_scale
    )
    far_exp = jnp.exp(far_scores)
    far_weights = far_exp / jnp.sum(far_exp, -1, keepdims=True)
    memory_blocks = jnp.einsum("hbqk,hbkd->hbqd", far_weights, far_values, precision=highest)
    memory_out = memory_blocks.reshape(heads_dev, shard_rows, head_width)
    mixed = gate_mix * local_out + (1.0 - gate_mix) * memory_out
    squares = lax.psum(jnp.sum(mixed * mixed, axis=(0, 2)), "head")
    feature_count = H * head_width
    inverse = lax.rsqrt(squares / feature_count + norm_eps)[None, :, None]
    shape = queries.shape
    head_base = lax.axis_index("head") * heads_dev
    token_base = blk_index * shard_rows
    counter = (
        (head_base + lax.broadcasted_iota(jnp.int32, shape, 0)) * (shard_rows * blk_count)
        + token_base
        + lax.broadcasted_iota(jnp.int32, shape, 1)
    ) * head_width + lax.broadcasted_iota(jnp.int32, shape, 2)
    keep = mix_bits(counter, drop_seed[0]).astype(jnp.float32)
    scaled_grad = norm_gain[:, None, :] * keep * out_grad
    slope = lax.psum(jnp.sum(scaled_grad * mixed, axis=(0, 2)), "head")
    mixed_grad = (
        inverse * scaled_grad
        - mixed * inverse * inverse * inverse * (slope / feature_count)[None, :, None]
    )
    near_grad = gate_mix * mixed_grad
    far_grad = ((1.0 - gate_mix) * mixed_grad).reshape(heads_dev, block_count, TB, head_width)
    far_delta = jnp.sum(far_grad * memory_blocks, -1, keepdims=True)
    far_dp = jnp.einsum("hbqd,hbkd->hbqk", far_grad, far_values, precision=highest)
    far_ds = far_weights * (far_dp - far_delta) * score_scale
    query_grad = jnp.einsum("hbqk,hbkd->hbqd", far_ds, far_keys, precision=highest).reshape(shape)
    tile_key_grad = jnp.einsum("hbqk,hbqd->hbkd", far_ds, query_blocks, precision=highest).reshape(
        heads_dev, slot_count, TB, head_width
    )
    tile_value_grad = jnp.einsum(
        "hbqk,hbqd->hbkd", far_weights, far_grad, precision=highest
    ).reshape(heads_dev, slot_count, TB, head_width)
    route = targets.astype(jnp.float32)
    send_key_grad = jnp.einsum("sj,hjtd->hstd", route, tile_key_grad, precision=highest)
    send_value_grad = jnp.einsum("sj,hjtd->hstd", route, tile_value_grad, precision=highest)
    back_key, back_value = (
        lax.all_to_all(send_key_grad, "blk", split_axis=1, concat_axis=1, tiled=True),
        lax.all_to_all(send_value_grad, "blk", split_axis=1, concat_axis=1, tiled=True),
    )
    owner_route = (jnp.arange(mb_dev, dtype=jnp.int32)[:, None] == asked[None, :]).astype(
        jnp.float32
    )
    memory_key_grad = jnp.einsum("ms,hstd->hmtd", owner_route, back_key, precision=highest).reshape(
        heads_dev, mb_dev * TB, head_width
    )
    memory_value_grad = jnp.einsum(
        "ms,hstd->hmtd", owner_route, back_value, precision=highest
    ).reshape(heads_dev, mb_dev * TB, head_width)
    near_delta = jnp.sum(near_grad * local_out, -1, keepdims=True)
    near_dp = jnp.einsum("hqd,hkd->hqk", near_grad, near_values, precision=highest)
    near_ds = near_weights * (near_dp - near_delta) * score_scale
    query_grad = query_grad + jnp.einsum("hqk,hkd->hqd", near_ds, near_keys, precision=highest)
    key_part = jnp.einsum("hqk,hqd->hkd", near_ds, queries, precision=highest)
    value_part = jnp.einsum("hqk,hqd->hkd", near_weights, near_grad, precision=highest)
    back_keys, back_values = from_behind(
        (key_part[:, :shard_rows], value_part[:, :shard_rows]), "blk", -1
    )
    key_grad = key_part[:, shard_rows:] + back_keys
    value_grad = value_part[:, shard_rows:] + back_values
    return (query_grad, key_grad, value_grad, memory_key_grad, memory_value_grad)


def solution(mesh):
    return jax.shard_map(
        local,
        mesh=mesh,
        in_specs=(
            P("head", "blk", None),
            P("head", "blk", None),
            P("head", "blk", None),
            P("head", "blk", None),
            P("head", "blk", None),
            P("head"),
            P("head", None),
            P("blk", None),
            P(),
            P("head", "blk", None),
        ),
        out_specs=(
            P("head", "blk", None),
            P("head", "blk", None),
            P("head", "blk", None),
            P("head", "blk", None),
            P("head", "blk", None),
        ),
        check_vma=False,
    )
```

profile of v0, /device:TPU:1, one launch (start us, length us, event | category | flops | bytes accessed | tf_op | source)
XLA Modules:
  0.0 547.2 jit_solution(999916907479044858)
XLA Ops:
  0.6 0.9 reshape.223
  1.9 9.0 %all_to_all.32 = s32[8,5,1]{1,2,0:T(1,128)S(1)} all-to-all(s32[8,5,1]{1,2,0:T(1,128)S(1)} %bitcast.104), channel_id=1, replica_groups=mesh['blk'=8,'head'=4] {'blk'}, dimensions={0} | all-to-all | bytes 320 | tf_op jit(solution)/shard_map/all_to_all | solution.py:83
  12.2 4.7 gather_fusion.2
  16.9 6.2 %gather_fusion = bf16[40,4,128,128]{3,2,1,0:T(8,128)(2,1)} fusion(bf16[4,16,128,128]{3,2,1,0:T(8,128)(2,1)} %bitcast.93, s32[1024]{0:T(1024)S(1)} %pad_clamp_fusion.1), kind=kCustom, calls=%fused_computation.clone | custom fusion | bytes 10485920 | tf_op jit(solution)/shard_map/jit(_take)/gather | solution.py:86
  23.1 9.0 %select_bitcast_fusion.1 = (bf16[4,40,128,128]{3,2,0,1:T(8,128)(2,1)}, bf16[4,40,128,128]{3,2,0,1:T(8,128)(2,1)}) fusion(bf16[40,4,128,128]{3,2,1,0:T(8,128)(2,1)} %gather_fusion, pred[40]{0:T(512)(128)(4,1)S(1)} %compare_and_fusion.1, bf16[40,4,128,128]{3,2,1,0:T(8,128)(2,1)} %gather_fusion.2), kind=kLoop, calls=%fused_computation.17 | loop fusion | flops 5242880 | bytes 20971560 | tf_op jit(solution)/shard_map/jit(_take)/select_n | solution.py:86
  32.0 64.3 %all_to_all.33 = bf16[4,40,128,128]{3,2,0,1:T(8,128)(2,1)} all-to-all(bf16[4,40,128,128]{3,2,0,1:T(8,128)(2,1)} %get-tuple-element.20), channel_id=1, replica_groups=mesh['blk'=8,'head'=4] {'blk'}, dimensions={1} | all-to-all | bytes 10485760 | tf_op jit(solution)/shard_map/all_to_all | solution.py:89
  96.3 6.0 %all-to-all-start.2 = ((bf16[4,40,128,128]{3,2,0,1:T(8,128)(2,1)}), bf16[4,40,128,128]{3,2,0,1:T(8,128)(2,1)}, u32[]{:S(2)}, u32[]{:S(2)}) async-start(bf16[4,40,128,128]{3,2,0,1:T(8,128)(2,1)} %get-tuple-element.21), calls=%async_computation.2 | async-start | bytes 10485760 | tf_op jit(solution)/shard_map/all_to_all | solution.py:90
  102.3 3.7 collective-permute-start
  106.0 2.1 collective-permute-start.1
  109.0 55.9 %collective-permute-done = f32[4,256,128]{2,1,0:T(8,128)} collective-permute-done((f32[4,256,128]{2,1,0:T(8,128)S(1)}, f32[4,256,128]{2,1,0:T(8,128)}, u32[]{:S(2)}, u32[]{:S(2)}) %collective-permute-start) | collective-permute-done | bytes 524320 | tf_op jit(solution)/shard_map/ppermute | solution.py:21
  164.9 1.1 constant_dynamic-update-slice_fusion.1
  166.0 4.5 collective-permute-done.1
  171.3 0.8 constant_dynamic-update-slice_fusion.2
  172.2 3.4 fusion.21
  175.6 5.6 %gather_fusion.1 = bf16[32,4,128,128]{3,2,1,0:T(8,128)(2,1)} fusion(bf16[4,40,128,128]{3,2,0,1:T(8,128)(2,1)} %all_to_all.33, s32[1024]{0:T(1024)S(1)} %pad_clamp_fusion), kind=kCustom, calls=%fused_computation.1.clone | custom fusion | bytes 8388736 | tf_op jit(solution)/shard_map/jit(_take)/gather | solution.py:93
  181.2 5.6 %gather_fusion.3 = bf16[32,4,128,128]{3,2,1,0:T(8,128)(2,1)} fusion(bf16[4,40,128,128]{3,2,0,1:T(8,128)(2,1)} %all-to-all-done.2, s32[1024]{0:T(1024)S(1)} %pad_clamp_fusion), kind=kCustom, calls=%fused_computation.3.clone | custom fusion | bytes 8388736 | tf_op jit(solution)/shard_map/jit(_take)/gather | solution.py:98
  186.8 4.1 select_bitcast_fusion.3
  191.8 1.7 copy-done.2
  193.5 4.4 bitcast_reduce_fusion
  198.0 7.6 %fusion.49 = f32[4,2,128,128]{3,2,1,0:T(8,128)S(1)} fusion(bf16[4,2,2048,128]{3,2,1,0:T(8,128)(2,1)S(1)} %bitcast.96, f32[4,2,2048,128]{3,2,1,0:T(8,128)S(1)} %get-tuple-element.27, f32[4,2,128]{2,1,0:T(2,128)S(1)} %get-tuple-element.26), kind=kOutput, calls=%fused_computation.93 | convolution fusion | flops 3225419776 | bytes 13111296 | tf_op jit(solution)/shard_map/hbqk,hbkd->hbqd/dot_general | solution.py:108
  205.6 6.1 %multiply_reduce_fusion.3 = (f32[256]{0:T(256)S(1)}, f32[256]{0:T(256)S(1)}, f32[4,256,128]{2,1,0:T(8,128)}, f32[4,256,128]{2,1,0:T(8,128)}) fusion(f32[4,256,128]{2,1,0:T(8,128)S(1)} %copy-done.13, s32[]{:T(128)} %bitcast.85, s32[4]{0:T(128)S(1)} %multiply_add_fusion, f32[4,128]{1,0:T(4,128)S(1)} %copy-done.14, f32[4,2,128,128]{3,2,1,0:T(8,128)S(1)} %fusion.49, ...), kind=kOutput, calls=%fused_computation.45 | convolution fusion | flops 810155520 | bytes 5382196 | tf_op jit(solution)/shard_map/hqk,hkd->hqd/dot_general | solution.py:66
  211.7 9.9 %all-reduce = (f32[256]{0:T(256)S(1)}, f32[256]{0:T(256)S(1)}) all-reduce(f32[256]{0:T(256)S(1)} %get-tuple-element.8, f32[256]{0:T(256)S(1)} %get-tuple-element.7), channel_id=1, replica_groups=mesh['blk'=8,'head'=4] {'head'}, use_global_device_ids=true, to_apply=%region_7.10 | all-reduce | flops 512 | bytes 4096 | tf_op jit(solution)/shard_map/psum | solution.py:124
  221.6 2.0 multiply_reduce_fusion
  224.1 7.8 %multiply_multiply_fusion = f32[4,2,128,2048]{2,3,1,0:T(8,128)S(1)} fusion(f32[4,2,128,128]{3,2,1,0:T(8,128)S(1)} %bitcast.101, bf16[4,2,2048,128]{3,2,1,0:T(8,128)(2,1)S(1)} %bitcast.97, f32[4,2,128]{2,1,0:T(2,128)S(1)} %multiply_reduce_fusion.1, f32[4,2,128]{2,1,0:T(2,128)S(1)} %get-tuple-element.26, f32[4,2,2048,128]{3,2,1,0:T(8,128)} %copy-done.5), kind=kOutput, calls=%fused_computation.14 | convolution fusion | flops 3231711232 | bytes 21504000 | tf_op jit(solution)/shard_map/hbqd,hbkd->hbqk/dot_general | solution.py:132
  231.9 8.8 %fusion.53 = f32[4,2,2048,128]{3,2,1,0:T(8,128)S(1)} fusion(f32[4,2,128,2048]{2,3,1,0:T(8,128)S(1)} %multiply_multiply_fusion, f32[4,2,128,128]{3,2,1,0:T(8,128)S(1)} %bitcast.95), kind=kOutput, calls=%fused_computation.96 | convolution fusion | flops 3221225472 | bytes 17301504 | tf_op jit(solution)/shard_map/hbqk,hbqd->hbkd/dot_general | solution.py:135
  240.7 10.7 %fusion.8 = f32[4,40,128,128]{3,1,2,0:T(8,128)S(1)} fusion(f32[4,32,128,128]{3,2,1,0:T(8,128)S(1)} %bitcast.87, s32[32]{0:T(128)S(1)} %get-tuple-element.17), kind=kOutput, calls=%fused_computation.20 | convolution fusion | flops 1006634240 | bytes 18874496 | tf_op jit(solution)/shard_map/sj,hjtd->hstd/dot_general | solution.py:142
  251.4 5.8 %copy.60 = f32[4,40,128,128]{3,2,0,1:T(8,128)} copy(f32[4,40,128,128]{3,1,2,0:T(8,128)S(1)} %fusion.8) | data formatting | bytes 20971520 | tf_op jit(solution)/shard_map/sj,hjtd->hstd/transpose | solution.py:142
  257.2 7.3 %all-to-all-start.3 = ((f32[4,40,128,128]{3,2,0,1:T(8,128)}), f32[4,40,128,128]{3,2,0,1:T(8,128)}, u32[]{:S(2)}, u32[]{:S(2)}) async-start(f32[4,40,128,128]{3,2,0,1:T(8,128)} %copy.60), calls=%async_computation.3 | async-start | bytes 20971520 | tf_op jit(solution)/shard_map/all_to_all | solution.py:145
  264.5 11.9 %fusion.48 = f32[4,2,2048,128]{3,2,1,0:T(8,128)S(1)} fusion(f32[4,2,128,128]{3,2,1,0:T(8,128)S(1)} %bitcast.102, f32[4,2,2048,128]{3,2,1,0:T(8,128)} %copy-done.5, f32[4,2,128]{2,1,0:T(2,128)S(1)} %get-tuple-element.26), kind=kOutput, calls=%fused_computation.92 | convolution fusion | flops 3225419776 | bytes 17305600 | tf_op jit(solution)/shard_map/hbqk,hbqd->hbkd/dot_general | solution.py:138
  276.4 10.4 %fusion.11 = f32[4,40,128,128]{3,1,2,0:T(8,128)S(1)} fusion(f32[4,32,128,128]{3,2,1,0:T(8,128)S(1)} %bitcast.92, s32[32]{0:T(128)S(1)} %get-tuple-element.17), kind=kOutput, calls=%fused_computation.21 | convolution fusion | flops 1006634240 | bytes 18874496 | tf_op jit(solution)/shard_map/sj,hjtd->hstd/dot_general | solution.py:143
  286.9 5.7 %copy.64 = f32[4,40,128,128]{3,2,0,1:T(8,128)} copy(f32[4,40,128,128]{3,1,2,0:T(8,128)S(1)} %fusion.11) | data formatting | bytes 20971520 | tf_op jit(solution)/shard_map/sj,hjtd->hstd/transpose | solution.py:143
  292.6 85.0 %all-to-all-done.3 = f32[4,40,128,128]{3,2,0,1:T(8,128)} async-done(((f32[4,40,128,128]{3,2,0,1:T(8,128)}), f32[4,40,128,128]{3,2,0,1:T(8,128)}, u32[]{:S(2)}, u32[]{:S(2)}) %all-to-all-start.3) | async-done | bytes 10485792 | tf_op jit(solution)/shard_map/all_to_all | solution.py:145
  377.6 8.8 %all-to-all-start.4 = ((f32[4,40,128,128]{3,2,0,1:T(8,128)}), f32[4,40,128,128]{3,2,0,1:T(8,128)}, u32[]{:S(2)}, u32[]{:S(2)}) async-start(f32[4,40,128,128]{3,2,0,1:T(8,128)} %copy.64), calls=%async_computation.4 | async-start | bytes 20971520 | tf_op jit(solution)/shard_map/all_to_all | solution.py:146
  386.4 4.1 fusion.29
  390.5 2.3 collective-permute-start.3
  392.9 3.8 multiply_multiply_fusion.1
  396.7 6.7 %fusion.51 = f32[4,2,128,128]{3,2,1,0:T(8,128)S(1)} fusion(f32[4,2,128,2048]{2,3,1,0:T(8,128)S(1)} %bitcast.91, bf16[4,2,2048,128]{3,2,1,0:T(8,128)(2,1)S(1)} %bitcast.89), kind=kOutput, calls=%fused_computation.94 | convolution fusion | flops 3221225472 | bytes 13107200 | tf_op jit(solution)/shard_map/hbqk,hbkd->hbqd/dot_general | solution.py:134
  403.4 1.9 fusion.52
  405.4 2.1 collective-permute-start.2
  407.5 4.2 convolution_add_fusion
  411.7 95.2 %collective-permute-done.3 = f32[4,256,128]{2,1,0:T(8,128)S(1)} collective-permute-done((f32[4,256,128]{2,1,0:T(8,128)S(1)}, f32[4,256,128]{2,1,0:T(8,128)S(1)}, u32[]{:S(2)}, u32[]{:S(2)}) %collective-permute-start.3) | collective-permute-done | bytes 524320 | tf_op jit(solution)/shard_map/ppermute | solution.py:21
  506.9 0.8 slice_add_fusion
  507.8 4.8 collective-permute-done.2
  512.5 0.9 slice_add_fusion.1
  513.4 13.2 %fusion.14 = f32[4,16,128,128]{3,1,2,0:T(8,128)S(1)} fusion(f32[4,40,128,128]{3,2,0,1:T(8,128)} %all-to-all-done.3, s32[40]{0:T(128)S(1)} %all_to_all.22), kind=kOutput, calls=%fused_computation.22 | convolution fusion | flops 503317120 | bytes 14680224 | tf_op jit(solution)/shard_map/ms,hstd->hmtd/dot_general | solution.py:151
  526.6 3.3 copy.62
  529.9 13.6 %fusion.17 = f32[4,16,128,128]{3,1,2,0:T(8,128)S(1)} fusion(f32[4,40,128,128]{3,2,0,1:T(8,128)} %all-to-all-done.4, s32[40]{0:T(128)S(1)} %all_to_all.22), kind=kOutput, calls=%fused_computation.23 | convolution fusion | flops 503317120 | bytes 14680224 | tf_op jit(solution)/shard_map/ms,hstd->hmtd/dot_general | solution.py:154
  543.5 3.3 copy.66
  (65 shorter events, 4.2 us)
Async XLA Ops:
  0.6 11.6 %copy-start = (bf16[4,2048,128]{2,1,0:T(8,128)(2,1)S(1)}, bf16[4,2048,128]{2,1,0:T(8,128)(2,1)}, u32[]{:S(2)}) copy-start(bf16[4,2048,128]{2,1,0:T(8,128)(2,1)} %param.18) | copy-start | bytes 6291460
  96.3 6.0 %copy-start.11 = (f32[4,256,128]{2,1,0:T(8,128)S(1)}, f32[4,256,128]{2,1,0:T(8,128)}, u32[]{:S(2)}) copy-start(f32[4,256,128]{2,1,0:T(8,128)} %param.15) | copy-start | bytes 1572868
  96.3 9.7 %copy-start.12 = (f32[4,256,128]{2,1,0:T(8,128)S(1)}, f32[4,256,128]{2,1,0:T(8,128)}, u32[]{:S(2)}) copy-start(f32[4,256,128]{2,1,0:T(8,128)} %param.16) | copy-start | bytes 1572868
  96.3 11.8 %copy-start.15 = (f32[4]{0:T(128)S(1)}, f32[4]{0:T(128)}, u32[]{:S(2)}) copy-start(f32[4]{0:T(128)} %param.19) | copy-start | bytes 52
  96.3 84.9 %all-to-all-start.2 = ((bf16[4,40,128,128]{3,2,0,1:T(8,128)(2,1)}), bf16[4,40,128,128]{3,2,0,1:T(8,128)(2,1)}, u32[]{:S(2)}, u32[]{:S(2)}) async-start(bf16[4,40,128,128]{3,2,0,1:T(8,128)(2,1)} %get-tuple-element.21), calls=%async_computation.2 | async-start | bytes 10485760 | tf_op jit(solution)/shard_map/all_to_all | solution.py:90
  102.3 69.9 %copy-start.6 = (f32[4,256,128]{2,1,0:T(8,128)S(1)}, f32[4,256,128]{2,1,0:T(8,128)}, u32[]{:S(2)}) copy-start(f32[4,256,128]{2,1,0:T(8,128)} %param.14) | copy-start | bytes 1572868
  102.3 62.6 %collective-permute-start = (f32[4,256,128]{2,1,0:T(8,128)S(1)}, f32[4,256,128]{2,1,0:T(8,128)}, u32[]{:S(2)}, u32[]{:S(2)}) collective-permute-start(f32[4,256,128]{2,1,0:T(8,128)S(1)} %copy-done.11), channel_id=1, source_target_pairs={{0,4},{4,8},{8,12},{12,16},{16,20},{20,24},{24,28},{1,5},{5,9},{9,... | collective-permute-start | bytes 1572872 | tf_op jit(solution)/shard_map/ppermute | solution.py:21
  106.0 64.5 %collective-permute-start.1 = (f32[4,256,128]{2,1,0:T(8,128)S(1)}, f32[4,256,128]{2,1,0:T(8,128)S(1)}, u32[]{:S(2)}, u32[]{:S(2)}) collective-permute-start(f32[4,256,128]{2,1,0:T(8,128)S(1)} %copy-done.12), channel_id=1, source_target_pairs={{0,4},{4,8},{8,12},{12,16},{16,20},{20,24},{24,28},{1,5},{5,9},{9,... | collective-permute-start | bytes 1572872 | tf_op jit(solution)/shard_map/ppermute | solution.py:21
  191.5 2.0 copy-start.2
  191.8 6.1 %copy-start.7 = (bf16[4,32,128,128]{3,2,1,0:T(8,128)(2,1)}, bf16[4,32,128,128]{3,2,1,0:T(8,128)(2,1)S(1)}, u32[]{:S(2)}) copy-start(bf16[4,32,128,128]{3,2,1,0:T(8,128)(2,1)S(1)} %copy.53) | copy-start | bytes 12582916
  198.0 7.6 %copy-start.5 = (f32[4,2,2048,128]{3,2,1,0:T(8,128)}, f32[4,2,2048,128]{3,2,1,0:T(8,128)S(1)}, u32[]{:S(2)}) copy-start(f32[4,2,2048,128]{3,2,1,0:T(8,128)S(1)} %get-tuple-element.27) | copy-start | bytes 25165828
  198.0 7.6 %copy-start.9 = (f32[4,512,256]{2,1,0:T(8,128)S(1)}, f32[4,512,256]{2,1,0:T(8,128)}, u32[]{:S(2)}) copy-start(f32[4,512,256]{2,1,0:T(8,128)} %get-tuple-element.25) | copy-start | bytes 6291460
  198.0 7.6 %copy-start.13 = (f32[4,256,128]{2,1,0:T(8,128)S(1)}, f32[4,256,128]{2,1,0:T(8,128)}, u32[]{:S(2)}) copy-start(f32[4,256,128]{2,1,0:T(8,128)} %param.23) | copy-start | bytes 1572868
  198.0 7.6 %copy-start.14 = (f32[4,128]{1,0:T(4,128)S(1)}, f32[4,128]{1,0:T(4,128)}, u32[]{:S(2)}) copy-start(f32[4,128]{1,0:T(4,128)} %param.20) | copy-start | bytes 6148
  221.6 2.5 copy-start.8
  231.9 8.8 %copy-start.4 = (f32[4,2,128,2048]{2,3,1,0:T(8,128)}, f32[4,2,128,2048]{2,3,1,0:T(8,128)S(1)}, u32[]{:S(2)}) copy-start(f32[4,2,128,2048]{2,3,1,0:T(8,128)S(1)} %multiply_multiply_fusion) | copy-start | bytes 25165828
  257.2 120.4 %all-to-all-start.3 = ((f32[4,40,128,128]{3,2,0,1:T(8,128)}), f32[4,40,128,128]{3,2,0,1:T(8,128)}, u32[]{:S(2)}, u32[]{:S(2)}) async-start(f32[4,40,128,128]{3,2,0,1:T(8,128)} %copy.60), calls=%async_computation.3 | async-start | bytes 20971520 | tf_op jit(solution)/shard_map/all_to_all | solution.py:145
  377.6 152.4 %all-to-all-start.4 = ((f32[4,40,128,128]{3,2,0,1:T(8,128)}), f32[4,40,128,128]{3,2,0,1:T(8,128)}, u32[]{:S(2)}, u32[]{:S(2)}) async-start(f32[4,40,128,128]{3,2,0,1:T(8,128)} %copy.64), calls=%async_computation.4 | async-start | bytes 20971520 | tf_op jit(solution)/shard_map/all_to_all | solution.py:146
  386.3 6.5 %copy-start.10 = (f32[4,512,256]{2,1,0:T(8,128)S(1)}, f32[4,512,256]{2,1,0:T(8,128)}, u32[]{:S(2)}) copy-start(f32[4,512,256]{2,1,0:T(8,128)} %get-tuple-element.25) | copy-start | bytes 6291460
  386.3 10.3 %slice-start = ((s8[8388608]{0:T(1024)(128)(4,1)}), s8[4194304]{0:T(1024)(128)(4,1)S(1)}, s32[]{:S(2)}) async-start(s8[8388608]{0:T(1024)(128)(4,1)} %bitcast.90), calls=%async_computation.5 | async-start | bytes 8388608
  390.5 6.2 %slice-start.1 = ((s8[8388608]{0:T(1024)(128)(4,1)}), s8[4194304]{0:T(1024)(128)(4,1)S(1)}, s32[]{:S(2)}) async-start(s8[8388608]{0:T(1024)(128)(4,1)} %bitcast.90), calls=%async_computation.6 | async-start | bytes 8388608
  390.5 116.4 %collective-permute-start.3 = (f32[4,256,128]{2,1,0:T(8,128)S(1)}, f32[4,256,128]{2,1,0:T(8,128)S(1)}, u32[]{:S(2)}, u32[]{:S(2)}) collective-permute-start(f32[4,256,128]{2,1,0:T(8,128)S(1)} %slice.27), channel_id=1, source_target_pairs={{4,0},{8,4},{12,8},{16,12},{20,16},{24,20},{28,24},{5,1},{9,5},{13... | collective-permute-start | bytes 1572872 | tf_op jit(solution)/shard_map/ppermute | solution.py:21
  392.9 3.8 copy-start.3
  405.4 107.2 %collective-permute-start.2 = (f32[4,256,128]{2,1,0:T(8,128)S(1)}, f32[4,256,128]{2,1,0:T(8,128)S(1)}, u32[]{:S(2)}, u32[]{:S(2)}) collective-permute-start(f32[4,256,128]{2,1,0:T(8,128)S(1)} %slice.25), channel_id=1, source_target_pairs={{4,0},{8,4},{12,8},{16,12},{20,16},{24,20},{28,24},{5,1},{9,5},{13... | collective-permute-start | bytes 1572872 | tf_op jit(solution)/shard_map/ppermute | solution.py:21
  529.9 16.9 %copy-start.1 = (bf16[4,2048,128]{2,1,0:T(8,128)(2,1)S(1)}, bf16[4,2048,128]{2,1,0:T(8,128)(2,1)}, u32[]{:S(2)}) copy-start(bf16[4,2048,128]{2,1,0:T(8,128)(2,1)} %param.18) | copy-start | bytes 6291460
where the time goes:
time: 554 us; the launch traced here: 547 us
  waiting for transfers between devices  245 us (44%)
  matrix products  119 us (21%)
  blocking collectives  83.2 us (15%)
  local copies, waits for them, and re-layouts  47.4 us (9%)
  starting transfers between devices  32.2 us (6%)
  other arithmetic  18.3 us (3%)
    ppermute x4, waiting for transfers between devices, from_behind(): return lax.ppermute(x, axis, pairs)  160 us
    all_to_all x1, waiting for transfers between devices, local(): lax.all_to_all(send_key_grad, 'blk', split_axis=1, concat_axis=1, tiled=T...  85 us
    all_to_all x1, blocking collectives, local(): lax.all_to_all(sent_keys, 'blk', split_axis=1, concat_axis=1, tiled=True)  64.3 us
    dot_general x1, matrix products, local(): jnp.einsum('ms,hstd->hmtd', owner_route, back_value, precision=highest)  13.6 us
    dot_general x1, matrix products, local(): jnp.einsum('ms,hstd->hmtd', owner_route, back_key, precision=highest)  13.2 us
    dot_general x1, matrix products, local(): jnp.einsum('hbqk,hbqd->hbkd', far_weights, far_grad, precision=highest)  11.9 us
  transfers between devices with their start and end apart: 7, of which 5 were waited for; matrix products, arithmetic and copies ran while one was open for 14% of the time, Pallas kernels for 0%

commit v1 on v0

v1 whole, which is shorter than its diff:
```python
import functools
import math

import jax
import jax.numpy as jnp
from jax import lax
from jax.experimental import pallas as pl
from jax.experimental.pallas import tpu as pltpu
from jax.sharding import PartitionSpec as P

H = 16
TB = 128
R = 16
EXTRA = 8

high = lax.Precision.HIGH
drop_level = 103
norm_eps = 1e-06
bf16 = jnp.bfloat16
f32 = jnp.float32


def from_behind(x, axis, by):
    devices = lax.axis_size(axis)
    pairs = [(i, i + by) for i in range(devices) if 0 <= i + by < devices]
    return lax.ppermute(x, axis, pairs)


def mix_bits(counter, seed_value):
    state = counter * jnp.int32(-1640531535) + seed_value
    state = state ^ lax.shift_right_logical(state, jnp.int32(15))
    state = state * jnp.int32(739982445)
    state = state ^ lax.shift_right_logical(state, jnp.int32(12))
    state = state * jnp.int32(695872825)
    state = state ^ lax.shift_right_logical(state, jnp.int32(15))
    return jnp.where(state & 1023 >= drop_level, 1.0 / 0.9, 0.0)


def split(x):
    top = x.astype(bf16)
    return top, (x - top.astype(f32)).astype(bf16)


def dot(a, b, ca, cb):
    return lax.dot_general(a, b, (((ca,), (cb,)), ((), ())), preferred_element_type=f32)


def collect_pairs(ids_ref, list_ref, mb_dev):
    me = lax.axis_index("blk")
    low = me * mb_dev

    def scan(i, count):
        list_ref[count] = i
        ident = ids_ref[i]
        mine = (ident >= low) & (ident < low + mb_dev)
        return count + mine.astype(jnp.int32)

    return lax.fori_loop(0, ids_ref.shape[0], scan, jnp.int32(0)), low


def place(ids_ref, list_ref, low, block_count, i):
    at = list_ref[i]
    block = at // R
    return block // block_count, (block % block_count) * TB, (ids_ref[at] - low) * TB, block % block_count


def far_forward(heads, mb_dev, block_count, scale, ids_ref, q_ref, k_ref, v_ref, out_ref, list_ref):
    out_ref[...] = jnp.zeros_like(out_ref)
    count, low = collect_pairs(ids_ref, list_ref, mb_dev)
    rows = q_ref.shape[2]
    ones = jnp.ones((8, 2 * TB), bf16)

    def step(i, carry):
        dev, q_at, k_at, sub = place(ids_ref, list_ref, low, block_count, i)
        q_rows = pl.ds(pl.multiple_of(q_at, TB), TB)
        k_rows = pl.ds(pl.multiple_of(k_at, TB), TB)
        for h in range(heads):
            q2 = jnp.concatenate(split(q_ref[dev, h, q_rows, :] * scale), 1)
            k = k_ref[h, k_rows, :]
            v = v_ref[h, k_rows, :]
            e = jnp.exp(dot(q2, jnp.concatenate([k, k], 1), 1, 1))
            e2 = jnp.concatenate(split(e), 1)
            out_ref[dev, h, q_rows, :] += dot(e2, jnp.concatenate([v, v], 0), 1, 0)
            out_ref[dev, h, pl.ds(rows + sub, 1), :] += dot(ones, e2, 1, 1)[:1]
        return carry

    lax.fori_loop(0, count, step, 0)


def far_backward(
    heads, mb_dev, block_count, scale, ids_ref, q_ref, g_ref, k_ref, v_ref, dq_ref, dk_ref, dv_ref, list_ref
):
    dq_ref[...] = jnp.zeros_like(dq_ref)
    dk_ref[...] = jnp.zeros_like(dk_ref)
    dv_ref[...] = jnp.zeros_like(dv_ref)
    count, low = collect_pairs(ids_ref, list_ref, mb_dev)
    rows = q_ref.shape[2]

    def step(i, carry):
        dev, q_at, k_at, sub = place(ids_ref, list_ref, low, block_count, i)
        q_rows = pl.ds(pl.multiple_of(q_at, TB), TB)
        k_rows = pl.ds(pl.multiple_of(k_at, TB), TB)
        for h in range(heads):
            qh, ql = split(q_ref[dev, h, q_rows, :] * scale)
            gh, gl = split(g_ref[dev, h, q_rows, :])
            delta = g_ref[dev, h, pl.ds(rows + sub, 1), :]
            rden = g_ref[dev, h, pl.ds(rows + block_count + sub, 1), :]
            k = k_ref[h, k_rows, :]
            v = v_ref[h, k_rows, :]
            st = dot(jnp.concatenate([k, k], 1), jnp.concatenate([qh, ql], 1), 1, 1)
            dp = dot(jnp.concatenate([v, v], 1), jnp.concatenate([gh, gl], 1), 1, 1)
            p = jnp.exp(st) * rden
            ds = p * (dp - delta)
            ph, plo = split(p)
            dh, dl = split(ds)
            dk_ref[h, k_rows, :] += dot(
                jnp.concatenate([dh, dl, dh], 1), jnp.concatenate([qh, qh, ql], 0), 1, 0
            )
            dv_ref[h, k_rows, :] += dot(
                jnp.concatenate([ph, plo, ph], 1), jnp.concatenate([gh, gh, gl], 0), 1, 0
            )
            dq_ref[dev, h, q_rows, :] += dot(
                jnp.concatenate([dh, dl], 0), jnp.concatenate([k, k], 0), 0, 0
            )
        return carry

    lax.fori_loop(0, count, step, 0)


def local(
    queries,
    key_rows,
    value_rows,
    memory_keys,
    memory_values,
    gate_bias,
    norm_gain,
    block_ids,
    drop_seed,
    out_grad,
):
    heads_dev, shard_rows, head_width = queries.shape
    block_count = shard_rows // TB
    score_scale = 1.0 / math.sqrt(head_width)
    blk_count = lax.axis_size("blk")
    blk_index = lax.axis_index("blk")
    mem_rows = memory_keys.shape[1]
    mb_dev = mem_rows // TB
    gate_mix = jax.nn.sigmoid(gate_bias)[:, None, None]
    hb = 2 if heads_dev % 2 == 0 else 1
    ids_all = lax.all_gather(block_ids.reshape(-1), "blk", axis=0, tiled=True)
    all_queries = lax.all_gather(queries, "blk", axis=0)
    prev_keys, prev_values = from_behind((key_rows, value_rows), "blk", 1)

    smem = pl.BlockSpec(memory_space=pltpu.SMEM)
    grid = (heads_dev // hb,)
    q_spec = pl.BlockSpec((blk_count, hb, shard_rows, head_width), lambda i: (0, i, 0, 0))
    x_spec = pl.BlockSpec((blk_count, hb, shard_rows + EXTRA, head_width), lambda i: (0, i, 0, 0))
    m_spec = pl.BlockSpec((hb, mem_rows, head_width), lambda i: (i, 0, 0))
    params = pltpu.CompilerParams(vmem_limit_bytes=56 * 1024 * 1024)
    scratch = [pltpu.SMEM((ids_all.shape[0] + 1,), jnp.int32)]
    tile_flops = 2 * TB * TB * head_width * heads_dev * block_count * R
    partial = pl.pallas_call(
        functools.partial(far_forward, hb, mb_dev, block_count, score_scale),
        grid=grid,
        in_specs=[smem, q_spec, m_spec, m_spec],
        out_specs=x_spec,
        out_shape=jax.ShapeDtypeStruct(
            (blk_count, heads_dev, shard_rows + EXTRA, head_width), f32
        ),
        scratch_shapes=scratch,
        compiler_params=params,
        cost_estimate=pl.CostEstimate(
            flops=8 * tile_flops, bytes_accessed=12 * 2**20, transcendentals=0
        ),
        name="far_forward",
    )(ids_all, all_queries, memory_keys, memory_values)

    near_keys = jnp.concatenate([prev_keys, key_rows], 1)
    near_values = jnp.concatenate([prev_values, value_rows], 1)
    row_pos = jnp.arange(shard_rows, dtype=jnp.int32)[:, None]
    col_pos = jnp.arange(2 * shard_rows, dtype=jnp.int32)[None, :]
    in_window = (
        (col_pos > row_pos)
        & (col_pos <= row_pos + shard_rows)
        & (blk_index * shard_rows - shard_rows + col_pos >= 0)
    )
    near_scores = jnp.einsum("hqd,hkd->hqk", queries, near_keys, precision=high) * score_scale
    near_exp = jnp.where(in_window[None], jnp.exp(near_scores), 0.0)
    near_total = jnp.sum(near_exp, -1, keepdims=True)
    near_weights = near_exp / near_total
    local_out = jnp.einsum("hqk,hkd->hqd", near_weights, near_values, precision=high)

    whole = lax.psum_scatter(partial, "blk", scatter_dimension=0, tiled=False)
    far_total = whole[:, shard_rows : shard_rows + block_count].reshape(heads_dev, shard_rows, 1)
    memory_out = whole[:, :shard_rows] / far_total

    mixed = gate_mix * local_out + (1.0 - gate_mix) * memory_out
    shape = queries.shape
    head_base = lax.axis_index("head") * heads_dev
    token_base = blk_index * shard_rows
    counter = (
        (head_base + lax.broadcasted_iota(jnp.int32, shape, 0)) * (shard_rows * blk_count)
        + token_base
        + lax.broadcasted_iota(jnp.int32, shape, 1)
    ) * head_width + lax.broadcasted_iota(jnp.int32, shape, 2)
    keep = mix_bits(counter, drop_seed[0]).astype(f32)
    scaled_grad = norm_gain[:, None, :] * keep * out_grad
    sums = lax.psum(
        jnp.stack([jnp.sum(mixed * mixed, axis=(0, 2)), jnp.sum(scaled_grad * mixed, axis=(0, 2))]),
        "head",
    )
    feature_count = H * head_width
    inverse = lax.rsqrt(sums[0] / feature_count + norm_eps)[None, :, None]
    mixed_grad = (
        inverse * scaled_grad
        - mixed * inverse * inverse * inverse * (sums[1] / feature_count)[None, :, None]
    )
    near_grad = gate_mix * mixed_grad
    far_grad = (1.0 - gate_mix) * mixed_grad
    far_delta = jnp.sum(far_grad * memory_out, -1)
    tail = jnp.concatenate(
        [
            far_delta.reshape(heads_dev, block_count, TB),
            (1.0 / far_total).reshape(heads_dev, block_count, TB),
            jnp.zeros((heads_dev, EXTRA - 2 * block_count, TB), f32),
        ],
        1,
    )
    all_grad = lax.all_gather(jnp.concatenate([far_grad, tail], 1), "blk", axis=0)
    dq_all, memory_key_grad, memory_value_grad = pl.pallas_call(
        functools.partial(far_backward, hb, mb_dev, block_count, score_scale),
        grid=grid,
        in_specs=[smem, q_spec, x_spec, m_spec, m_spec],
        out_specs=[q_spec, m_spec, m_spec],
        out_shape=[
            jax.ShapeDtypeStruct((blk_count, heads_dev, shard_rows, head_width), f32),
            jax.ShapeDtypeStruct((heads_dev, mem_rows, head_width), f32),
            jax.ShapeDtypeStruct((heads_dev, mem_rows, head_width), f32),
        ],
        scratch_shapes=scratch,
        compiler_params=params,
        cost_estimate=pl.CostEstimate(
            flops=24 * tile_flops, bytes_accessed=24 * 2**20, transcendentals=0
        ),
        name="far_backward",
    )(ids_all, all_queries, all_grad, memory_keys, memory_values)
    far_query_grad = lax.psum_scatter(dq_all, "blk", scatter_dimension=0, tiled=False) * score_scale

    near_delta = jnp.sum(near_grad * local_out, -1, keepdims=True)
    near_dp = jnp.einsum("hqd,hkd->hqk", near_grad, near_values, precision=high)
    near_ds = near_weights * (near_dp - near_delta) * score_scale
    key_part = jnp.einsum("hqk,hqd->hkd", near_ds, queries, precision=high)
    value_part = jnp.einsum("hqk,hqd->hkd", near_weights, near_grad, precision=high)
    back_keys, back_values = from_behind(
        (key_part[:, :shard_rows], value_part[:, :shard_rows]), "blk", -1
    )
    key_grad = key_part[:, shard_rows:] + back_keys
    value_grad = value_part[:, shard_rows:] + back_values
    near_query_grad = jnp.einsum("hqk,hkd->hqd", near_ds, near_keys, precision=high)
    query_grad = near_query_grad + far_query_grad
    return (query_grad, key_grad, value_grad, memory_key_grad, memory_value_grad)


def solution(mesh):
    return jax.shard_map(
        local,
        mesh=mesh,
        in_specs=(
            P("head", "blk", None),
            P("head", "blk", None),
            P("head", "blk", None),
            P("head", "blk", None),
            P("head", "blk", None),
            P("head"),
            P("head", None),
            P("blk", None),
            P(),
            P("head", "blk", None),
        ),
        out_specs=(
            P("head", "blk", None),
            P("head", "blk", None),
            P("head", "blk", None),
            P("head", "blk", None),
            P("head", "blk", None),
        ),
        check_vma=False,
    )
```

time: 554 us -> 315 us (0.57)
  matrix products: 119 us -> 15.9 us
  waiting for transfers between devices: 245 us -> 151 us
  Pallas kernels: 0 us -> 81.4 us
  blocking collectives: 83.2 us -> 17.5 us
  local copies, waits for them, and re-layouts: 47.4 us -> 5.17 us
  between operations: 2.18 us -> 15.3 us
  starting transfers between devices: 32.2 us -> 19.4 us
  other arithmetic: 18.3 us -> 7.79 us
    ppermute x4, waiting for transfers between devices: 160 us -> 16.1 us  [from_behind(): return lax.ppermute(x, axis, pairs)]
    dot_general x16 -> x6, matrix products: 119 us -> 15.9 us  [the longest x1 4.58 us: local(): jnp.einsum('hqk,hkd->hqd', near_weights, near_values, precision=high)]
    all_to_all x3 -> x0, waiting for transfers between devices: 85 us -> none  [the longest x1 85 us: local(): lax.all_to_all(send_key_grad, 'blk', split_axis=1, concat_axis=1, tiled=T...]
    pallas_call x0 -> x2, Pallas kernels: none -> 81.4 us  [the longest x1 51 us: local(): pl.pallas_call(functools.partial(far_backward, hb, mb_dev, block_count, s...]
    all_to_all x2 -> x0, blocking collectives: 73.3 us -> none  [the longest x1 64.3 us: local(): lax.all_to_all(sent_keys, 'blk', split_axis=1, concat_axis=1, tiled=True)]
    all_gather x0 -> x2, waiting for transfers between devices: none -> 67.5 us  [the longest x1 37 us: local(): lax.all_gather(jnp.concatenate([far_grad, tail], 1), 'blk', axis=0)]
    reduce_scatter x0 -> x2, waiting for transfers between devices: none -> 66.5 us  [the longest x1 33.5 us: local(): whole = lax.psum_scatter(partial, 'blk', scatter_dimension=0, tiled=False)]
    all_to_all x3 -> x0, starting transfers between devices: 22.1 us -> none  [the longest x1 8.77 us: local(): lax.all_to_all(send_value_grad, 'blk', split_axis=1, concat_axis=1, tiled...]
  transfers between devices with their start and end apart: 7 -> 8, of which waited for: 5 -> 8; matrix products, arithmetic and copies ran while one was open for 14% -> 4% of each run, Pallas kernels for 0% -> 0%
where the time goes in v1:
time: 315 us; the launch traced here: 313 us
  waiting for transfers between devices  151 us (48%)
  Pallas kernels  81.4 us (26%)
  starting transfers between devices  19.4 us (6%)
  blocking collectives  17.5 us (6%)
  matrix products  15.9 us (5%)
  between operations  15.3 us (5%)
  other arithmetic  7.79 us (2%)
  local copies, waits for them, and re-layouts  5.17 us (2%)
    pallas_call x1, Pallas kernels, local(): pl.pallas_call(functools.partial(far_backward, hb, mb_dev, block_count, s...  51 us
    all_gather x1, waiting for transfers between devices, local(): lax.all_gather(jnp.concatenate([far_grad, tail], 1), 'blk', axis=0)  37 us
    reduce_scatter x1, waiting for transfers between devices, local(): whole = lax.psum_scatter(partial, 'blk', scatter_dimension=0, tiled=False)  33.5 us
    reduce_scatter x1, waiting for transfers between devices, local(): lax.psum_scatter(dq_all, 'blk', scatter_dimension=0, tiled=False)  33 us
    all_gather x1, waiting for transfers between devices, local(): all_queries = lax.all_gather(queries, 'blk', axis=0)  30.5 us
    pallas_call x1, Pallas kernels, local(): pl.pallas_call(functools.partial(far_forward, hb, mb_dev, block_count, sc...  30.4 us
    ppermute x4, starting transfers between devices, from_behind(): return lax.ppermute(x, axis, pairs)  19.3 us
    ppermute x4, waiting for transfers between devices, from_behind(): return lax.ppermute(x, axis, pairs)  16.1 us
  transfers between devices with their start and end apart: 8, of which 8 were waited for; matrix products, arithmetic and copies ran while one was open for 4% of the time, Pallas kernels for 0%

profile of v1, /device:TPU:1, one launch (start us, length us, event | category | flops | bytes accessed | tf_op | source)
XLA Modules:
  0.0 313.4 jit_solution(6375492323469941002)
XLA Ops:
  7.2 0.0 all-gather.5.cloned.1.call-start
  7.2 0.7 all-gather.5.cloned.1.call-update
  7.9 0.0 reduce-scatter.3.cloned.1.call-start
  8.0 0.8 reshape.112
  8.7 1.2 dynamic-slice
  10.6 0.2 dynamic-update-slice
  10.9 7.8 %all-reduce.ids_ref = s32[256]{0:T(256)} all-reduce(s32[256]{0:T(256)S(1)} %dynamic-update-slice), channel_id=1, replica_groups=mesh['blk'=8,'head'=4] {'blk'}, use_global_device_ids=true, to_apply=%add | all-reduce | flops 256 | bytes 2048
  18.7 30.5 %all-gather.5.cloned.1.call-done = f32[32,256,128]{2,1,0:T(8,128)} async-done(((f32[4,256,128]{2,1,0:T(8,128)}), f32[32,256,128]{2,1,0:T(8,128)}) %all-gather.5.cloned.1.call-update) | async-done | bytes 4194320 | tf_op jit(solution)/shard_map/all_gather | solution.py:152
  49.1 30.4 %far_forward.1 = f32[8,4,264,128]{3,2,1,0:T(8,128)} custom-call(s32[256]{0:T(256)} %all-reduce.ids_ref, f32[8,4,256,128]{3,2,1,0:T(8,128)} %bitcast.48, bf16[4,2048,128]{2,1,0:T(8,128)(2,1)} %k_ref.3, bf16[4,2048,128]{2,1,0:T(8,128)(2,1)} %v_ref.3), custom_call_target="tpu_custom_call" | custom-call | flops 4294967296 | bytes 12582912 | tf_op jit(solution)/shard_map/far_forward/pallas_call | solution.py:163
  79.5 0.0 reduce-scatter.3.cloned.1.call-update
  79.6 0.0 all-gather.7.cloned.1.call-start
  79.6 1.0 copy-done.5
  80.6 6.9 %collective-permute-start = (f32[4,256,128]{2,1,0:T(8,128)S(1)}, f32[4,256,128]{2,1,0:T(8,128)S(1)}, u32[]{:S(2)}, u32[]{:S(2)}) collective-permute-start(f32[4,256,128]{2,1,0:T(8,128)S(1)} %copy-done.5), channel_id=1, source_target_pairs={{0,4},{4,8},{8,12},{12,16},{16,20},{20,24},{24,28},{1,5},{5,9},{9,... | collective-permute-start | bytes 1572872 | tf_op jit(solution)/shard_map/ppermute | solution.py:26
  87.5 2.9 collective-permute-start.1
  91.1 0.1 pad.3.clone
  91.2 0.2 fusion.7
  91.4 0.0 copy-start
  91.4 2.2 collective-permute-done
  93.7 5.5 %collective-permute-done.1 = f32[4,256,128]{2,1,0:T(8,128)S(1)} collective-permute-done((f32[4,256,128]{2,1,0:T(8,128)S(1)}, f32[4,256,128]{2,1,0:T(8,128)S(1)}, u32[]{:S(2)}, u32[]{:S(2)}) %collective-permute-start.1) | collective-permute-done | bytes 524320 | tf_op jit(solution)/shard_map/ppermute | solution.py:26
  99.2 0.8 constant_dynamic-update-slice_fusion.3
  100.0 0.8 constant_dynamic-update-slice_fusion.2
  100.9 1.3 fusion.1
  102.2 33.5 %reduce-scatter.3.cloned.1.call-done = f32[1,4,264,128]{3,2,1,0:T(8,128)} async-done(((f32[8,4,264,128]{3,2,1,0:T(8,128)}), f32[1,4,264,128]{3,2,1,0:T(8,128)}) %reduce-scatter.3.cloned.1.call-update) | async-done | bytes 540688 | tf_op jit(solution)/shard_map/reduce_scatter | solution.py:194
  135.7 0.7 slice_divide_fusion.1
  136.4 4.6 %multiply_reduce_fusion.3 = (f32[256]{0:T(256)S(1)}, f32[256]{0:T(256)S(1)}, f32[4,256,128]{2,1,0:T(8,128)}, f32[4,256,128]{2,1,0:T(8,128)}) fusion(f32[4,256,128]{2,1,0:T(8,128)} %param.19, s32[]{:T(128)} %bitcast.36, s32[4]{0:T(128)S(1)} %multiply_add_fusion.1, f32[4,128]{1,0:T(4,128)S(1)} %copy-done.8, f32[4,256]{1,0:T(4,128)S(1)} %bitcast.41, ...), kind=kOutput, calls=%fused_computation.21 | convolution fusion | flops 407633408 | bytes 5386292 | tf_op jit(solution)/shard_map/hqk,hkd->hqd/dot_general | solution.py:192
  141.0 9.7 %psum.7 = f32[2,256]{1,0:T(2,128)S(1)} all-reduce(f32[2,256]{1,0:T(2,128)S(1)} %pad_maximum_fusion), channel_id=1, replica_groups=mesh['blk'=8,'head'=4] {'head'}, use_global_device_ids=true, to_apply=%region_4.5 | all-reduce | flops 512 | bytes 4096 | tf_op jit(solution)/shard_map/psum | solution.py:209
  150.7 2.9 multiply_reduce_fusion
  153.6 1.9 maximum_maximum_fusion
  155.6 0.0 all-gather.7.cloned.1.call-update
  155.6 0.0 reduce-scatter.5.cloned.1.call-start
  155.6 37.0 %all-gather.7.cloned.1.call-done = f32[32,264,128]{2,1,0:T(8,128)} async-done(((f32[4,264,128]{2,1,0:T(8,128)}), f32[32,264,128]{2,1,0:T(8,128)}) %all-gather.7.cloned.1.call-update) | async-done | bytes 4325392 | tf_op jit(solution)/shard_map/all_gather | solution.py:230
  192.7 51.0 %far_backward.1 = (f32[8,4,256,128]{3,2,1,0:T(8,128)}, f32[4,2048,128]{2,1,0:T(8,128)}, f32[4,2048,128]{2,1,0:T(8,128)}) custom-call(s32[256]{0:T(256)} %all-reduce.ids_ref, f32[8,4,256,128]{3,2,1,0:T(8,128)} %bitcast.49, f32[8,4,264,128]{3,2,1,0:T(8,128)} %bitcast.47, bf16[4,2048,128]{2,1,0:T(8,128)(2,1)} %k_ref.3, bf16[4,2048,128]{2,1,0:T(8,128)(2,1)} %v_ref.3), custom_call_target="tpu_custom_call" | custom-call | flops 12884901888 | bytes 25165824 | tf_op jit(solution)/shard_map/far_backward/pallas_call | solution.py:231
  243.7 0.0 reduce-scatter.5.cloned.1.call-update
  243.7 0.0 copy-start.4
  243.8 0.0 copy-start.7
  243.8 2.5 fusion.8
  246.3 7.6 %collective-permute-start.3 = (f32[4,256,128]{2,1,0:T(8,128)S(1)}, f32[4,256,128]{2,1,0:T(8,128)S(1)}, u32[]{:S(2)}, u32[]{:S(2)}) collective-permute-start(f32[4,256,128]{2,1,0:T(8,128)S(1)} %slice.39), channel_id=1, source_target_pairs={{4,0},{8,4},{12,8},{16,12},{20,16},{24,20},{28,24},{5,1},{9,5},{13... | collective-permute-start | bytes 1572872 | tf_op jit(solution)/shard_map/ppermute | solution.py:26
  253.9 0.3 multiply_reduce_fusion.1
  254.2 0.0 copy-start.1
  254.2 2.9 multiply_multiply_fusion
  257.1 1.0 fusion.18
  258.1 1.9 collective-permute-start.2
  260.1 3.0 collective-permute-done.3
  263.1 0.8 slice_add_fusion
  263.9 5.3 %collective-permute-done.2 = f32[4,256,128]{2,1,0:T(8,128)S(1)} collective-permute-done((f32[4,256,128]{2,1,0:T(8,128)S(1)}, f32[4,256,128]{2,1,0:T(8,128)S(1)}, u32[]{:S(2)}, u32[]{:S(2)}) %collective-permute-start.2) | collective-permute-done | bytes 524320 | tf_op jit(solution)/shard_map/ppermute | solution.py:26
  269.3 0.9 slice_add_fusion.1
  270.2 33.0 %reduce-scatter.5.cloned.1.call-done = f32[1,4,256,128]{3,2,1,0:T(8,128)} async-done(((f32[8,4,256,128]{3,2,1,0:T(8,128)}), f32[1,4,256,128]{3,2,1,0:T(8,128)}) %reduce-scatter.5.cloned.1.call-update) | async-done | bytes 524304 | tf_op jit(solution)/shard_map/reduce_scatter | solution.py:248
  303.2 3.6 %convolution_add_fusion = f32[4,256,128]{2,1,0:T(8,128)} fusion(f32[4,256,512]{1,2,0:T(8,128)S(1)} %multiply_multiply_fusion, f32[4,512,128]{2,1,0:T(8,128)S(1)} %constant_dynamic-update-slice_fusion, f32[1,4,256,128]{3,2,1,0:T(8,128)} %reduce-scatter.5.cloned.1.call-done), kind=kOutput, calls=%fused_computation.4 | convolution fusion | flops 402915328 | bytes 4194304 | tf_op jit(solution)/shard_map/hqk,hkd->hqd/dot_general | solution.py:260
  (29 shorter events, 0.2 us)
Async XLA Ops:
  7.2 42.0 %all-gather.5.cloned.1.call-start = ((), (), s32[]{:S(2)}) async-start(), calls=%async_computation.4 | async-start | bytes 4718592 | tf_op jit(solution)/shard_map/all_gather | solution.py:152
  7.9 127.8 %reduce-scatter.3.cloned.1.call-start = ((), (), s32[]{:S(2)}) async-start(), calls=%async_computation.2 | async-start | bytes 4866048 | tf_op jit(solution)/shard_map/reduce_scatter | solution.py:194
  79.5 1.0 copy-start.5
  79.5 7.9 %copy-start.6 = (f32[4,256,128]{2,1,0:T(8,128)S(1)}, f32[4,256,128]{2,1,0:T(8,128)}, u32[]{:S(2)}) copy-start(f32[4,256,128]{2,1,0:T(8,128)} %param.12) | copy-start | bytes 1572868
  79.5 10.9 %copy-start.9 = (f32[4]{0:T(128)S(1)}, f32[4]{0:T(128)}, u32[]{:S(2)}) copy-start(f32[4]{0:T(128)} %param.15) | copy-start | bytes 52
  79.6 113.1 %all-gather.7.cloned.1.call-start = ((), (), s32[]{:S(2)}) async-start(), calls=%async_computation.5 | async-start | bytes 4866048 | tf_op jit(solution)/shard_map/all_gather | solution.py:230
  80.6 13.0 %collective-permute-start = (f32[4,256,128]{2,1,0:T(8,128)S(1)}, f32[4,256,128]{2,1,0:T(8,128)S(1)}, u32[]{:S(2)}, u32[]{:S(2)}) collective-permute-start(f32[4,256,128]{2,1,0:T(8,128)S(1)} %copy-done.5), channel_id=1, source_target_pairs={{0,4},{4,8},{8,12},{12,16},{16,20},{20,24},{24,28},{1,5},{5,9},{9,... | collective-permute-start | bytes 1572872 | tf_op jit(solution)/shard_map/ppermute | solution.py:26
  87.5 11.7 %collective-permute-start.1 = (f32[4,256,128]{2,1,0:T(8,128)S(1)}, f32[4,256,128]{2,1,0:T(8,128)S(1)}, u32[]{:S(2)}, u32[]{:S(2)}) collective-permute-start(f32[4,256,128]{2,1,0:T(8,128)S(1)} %copy-done.6), channel_id=1, source_target_pairs={{0,4},{4,8},{8,12},{12,16},{16,20},{20,24},{24,28},{1,5},{5,9},{9,... | collective-permute-start | bytes 1572872 | tf_op jit(solution)/shard_map/ppermute | solution.py:26
  91.4 9.5 %copy-start = (f32[4,256,128]{2,1,0:T(8,128)S(1)}, f32[4,256,128]{2,1,0:T(8,128)}, u32[]{:S(2)}) copy-start(f32[4,256,128]{2,1,0:T(8,128)} %param.10) | copy-start | bytes 1572868
  100.9 35.5 %copy-start.8 = (f32[4,128]{1,0:T(4,128)S(1)}, f32[4,128]{1,0:T(4,128)}, u32[]{:S(2)}) copy-start(f32[4,128]{1,0:T(4,128)} %param.16) | copy-start | bytes 6148
  102.2 141.5 %copy-start.2 = (f32[4,512,256]{2,1,0:T(8,128)}, f32[4,512,256]{2,1,0:T(8,128)S(1)}, u32[]{:S(2)}) copy-start(f32[4,512,256]{2,1,0:T(8,128)S(1)} %get-tuple-element.24) | copy-start | bytes 6291460
  155.6 147.6 %reduce-scatter.5.cloned.1.call-start = ((), (), s32[]{:S(2)}) async-start(), calls=%async_computation.3 | async-start | bytes 4718592 | tf_op jit(solution)/shard_map/reduce_scatter | solution.py:248
  243.7 10.1 %copy-start.4 = (f32[4,256,128]{2,1,0:T(8,128)S(1)}, f32[4,256,128]{2,1,0:T(8,128)}, u32[]{:S(2)}) copy-start(f32[4,256,128]{2,1,0:T(8,128)} %get-tuple-element.15) | copy-start | bytes 1572868
  243.8 10.1 %copy-start.7 = (f32[4,256,128]{2,1,0:T(8,128)S(1)}, f32[4,256,128]{2,1,0:T(8,128)}, u32[]{:S(2)}) copy-start(f32[4,256,128]{2,1,0:T(8,128)} %get-tuple-element.25) | copy-start | bytes 1572868
  246.2 7.9 %copy-start.3 = (f32[4,512,256]{2,1,0:T(8,128)S(1)}, f32[4,512,256]{2,1,0:T(8,128)}, u32[]{:S(2)}) copy-start(f32[4,512,256]{2,1,0:T(8,128)} %copy-done.2) | copy-start | bytes 6291460
  246.3 16.8 %collective-permute-start.3 = (f32[4,256,128]{2,1,0:T(8,128)S(1)}, f32[4,256,128]{2,1,0:T(8,128)S(1)}, u32[]{:S(2)}, u32[]{:S(2)}) collective-permute-start(f32[4,256,128]{2,1,0:T(8,128)S(1)} %slice.39), channel_id=1, source_target_pairs={{4,0},{8,4},{12,8},{16,12},{20,16},{24,20},{28,24},{5,1},{9,5},{13... | collective-permute-start | bytes 1572872 | tf_op jit(solution)/shard_map/ppermute | solution.py:26
  254.2 2.9 copy-start.1
  258.1 11.2 %collective-permute-start.2 = (f32[4,256,128]{2,1,0:T(8,128)S(1)}, f32[4,256,128]{2,1,0:T(8,128)S(1)}, u32[]{:S(2)}, u32[]{:S(2)}) collective-permute-start(f32[4,256,128]{2,1,0:T(8,128)S(1)} %slice.37), channel_id=1, source_target_pairs={{4,0},{8,4},{12,8},{16,12},{20,16},{24,20},{28,24},{5,1},{9,5},{13... | collective-permute-start | bytes 1572872 | tf_op jit(solution)/shard_map/ppermute | solution.py:26
Sparse Core Ops, SparseCore 0:
  9.9 39.2 all-gather.4
  79.7 55.9 reduce-scatter.2
  155.7 36.9 all-gather.6
  243.9 59.2 reduce-scatter.4

commit v2 on v1

--- a/solution.py
+++ b/solution.py
@@ -45,28 +45,222 @@
     return lax.dot_general(a, b, (((ca,), (cb,)), ((), ())), preferred_element_type=f32)
 
 
-def collect_pairs(ids_ref, list_ref, mb_dev):
+def flip(index, bit):
+    return index + bit - 2 * bit * ((index // bit) % 2)
+
+
+def greet(others):
+    barrier = pltpu.get_barrier_semaphore()
+    for other in others:
+        pl.semaphore_signal(
+            barrier, inc=1, device_id={"blk": other}, device_id_type=pl.DeviceIdType.MESH
+        )
+    pl.semaphore_wait(barrier, len(others))
+
+
+def sender(send_sems, recv_sems):
+    def send(src, dst, index, other):
+        copy = pltpu.make_async_remote_copy(
+            src_ref=src,
+            dst_ref=dst,
+            send_sem=send_sems.at[index],
+            recv_sem=recv_sems.at[index],
+            device_id={"blk": other},
+            device_id_type=pl.DeviceIdType.MESH,
+        )
+        copy.start()
+        return copy
+
+    return send
+
+
+def gather_steps(x_ref, out_ref, send_sems, recv_sems, own_sem):
+    me = lax.axis_index("blk")
+    side, over_x, over_y = flip(me, 1), flip(me, 2), flip(me, 4)
+    far = flip(over_x, 4)
+    half = x_ref.shape[0] // 2
+    low, high_part = pl.ds(0, half), pl.ds(half, half)
+    send = sender(send_sems, recv_sems)
+    to_x = send(x_ref, out_ref.at[me], 1, over_x)
+    to_y = send(x_ref, out_ref.at[me], 2, over_y)
+    to_side = send(x_ref, out_ref.at[me], 0, side)
+    own = pltpu.make_async_copy(x_ref, out_ref.at[me], own_sem)
+    own.start()
+    to_x.wait_recv()
+    x_to_y = send(out_ref.at[over_x, high_part], out_ref.at[over_x, high_part], 4, over_y)
+    x_to_side = send(out_ref.at[over_x], out_ref.at[over_x], 3, side)
+    to_y.wait_recv()
+    y_to_x = send(out_ref.at[over_y, low], out_ref.at[over_y, low], 6, over_x)
+    y_to_side = send(out_ref.at[over_y], out_ref.at[over_y], 5, side)
+    y_to_x.wait_recv()
+    low_to_side = send(out_ref.at[far, low], out_ref.at[far, low], 7, side)
+    x_to_y.wait_recv()
+    high_to_side = send(out_ref.at[far, high_part], out_ref.at[far, high_part], 8, side)
+    for copy in (to_side, x_to_side, y_to_side, low_to_side, high_to_side):
+        copy.wait()
+    for copy in (to_x, to_y, x_to_y, y_to_x):
+        copy.wait_send()
+    own.wait()
+
+
+def gather_ids_kernel(x_ref, ids_ref, out_ref, ids_out_ref, send_sems, recv_sems, id_send, id_recv, own_sems):
+    me = lax.axis_index("blk")
+    count = out_ref.shape[0]
+    others = [(me + j) % count for j in range(1, count)]
+    greet(others)
+    own = pltpu.make_async_copy(ids_ref, ids_out_ref.at[me], own_sems.at[1])
+    own.start()
+    send = sender(id_send, id_recv)
+    copies = [send(ids_ref, ids_out_ref.at[me], j, other) for j, other in enumerate(others)]
+    gather_steps(x_ref, out_ref, send_sems, recv_sems, own_sems.at[0])
+    for copy in copies:
+        copy.wait()
+    own.wait()
+
+
+def gather_kernel(x_ref, out_ref, send_sems, recv_sems, own_sem):
+    me = lax.axis_index("blk")
+    greet([flip(me, 1), flip(me, 2), flip(me, 4)])
+    gather_steps(x_ref, out_ref, send_sems, recv_sems, own_sem)
+
+
+def gather_blocks(x, collective_id, ids=None):
+    count = lax.axis_size("blk")
+    if count != 8 or x.shape[0] % 2:
+        gathered = lax.all_gather(x, "blk", axis=0)
+        return gathered if ids is None else (gathered, lax.all_gather(ids, "blk", axis=0))
+    whole = jax.ShapeDtypeStruct((count,) + x.shape, x.dtype)
+    any_space = pl.BlockSpec(memory_space=pl.ANY)
+    params = pltpu.CompilerParams(collective_id=collective_id, has_side_effects=True)
+    sems = [pltpu.SemaphoreType.DMA((9,)), pltpu.SemaphoreType.DMA((9,))]
+    cost = pl.CostEstimate(flops=0, bytes_accessed=2**26, transcendentals=0)
+    if ids is None:
+        return pl.pallas_call(
+            gather_kernel,
+            in_specs=[any_space],
+            out_specs=any_space,
+            out_shape=whole,
+            scratch_shapes=sems + [pltpu.SemaphoreType.DMA],
+            compiler_params=params,
+            cost_estimate=cost,
+            name="gather_grad",
+        )(x)
+    return pl.pallas_call(
+        gather_ids_kernel,
+        in_specs=[any_space, pl.BlockSpec(memory_space=pltpu.VMEM)],
+        out_specs=[any_space, pl.BlockSpec(memory_space=pltpu.VMEM)],
+        out_shape=[whole, jax.ShapeDtypeStruct((count,) + ids.shape, ids.dtype)],
+        scratch_shapes=sems
+        + [
+            pltpu.SemaphoreType.DMA((count - 1,)),
+            pltpu.SemaphoreType.DMA((count - 1,)),
+            pltpu.SemaphoreType.DMA((2,)),
+        ],
+        compiler_params=params,
+        cost_estimate=cost,
+        name="gather_queries",
+    )(x, ids)
+
+
+def scatter_kernel(
+    part_ref, out_ref, side_ref, far_ref, x_ref, y_ref, hop_ref, in_x_ref, in_y_ref, send_sems, recv_sems
+):
+    me = lax.axis_index("blk")
+    side, over_x, over_y = flip(me, 1), flip(me, 2), flip(me, 4)
+    far = flip(over_x, 4)
+    half = out_ref.shape[0] // 2
+    low, high_part = pl.ds(0, half), pl.ds(half, half)
+    greet([side, over_x, over_y])
+    send = sender(send_sems, recv_sems)
+    far_in = send(part_ref.at[flip(far, 1)], side_ref.at[0], 0, side)
+    x_in = send(part_ref.at[flip(over_x, 1)], side_ref.at[1], 1, side)
+    y_in = send(part_ref.at[flip(over_y, 1)], side_ref.at[2], 2, side)
+    own_in = send(part_ref.at[side], side_ref.at[3], 3, side)
+    far_in.wait_recv()
+    far_ref[...] = part_ref[far] + side_ref[0]
+    far_to_x = send(far_ref.at[low], hop_ref.at[0], 4, over_x)
+    far_to_y = send(far_ref.at[high_part], hop_ref.at[1], 5, over_y)
+    x_in.wait_recv()
+    x_ref[...] = part_ref[over_x] + side_ref[1]
+    x_low = send(x_ref.at[low], in_x_ref.at[low], 6, over_x)
+    y_in.wait_recv()
+    y_ref[...] = part_ref[over_y] + side_ref[2]
+    y_high = send(y_ref.at[high_part], in_y_ref.at[high_part], 7, over_y)
+    far_to_y.wait_recv()
+    x_ref[high_part] += hop_ref[1]
+    x_high = send(x_ref.at[high_part], in_x_ref.at[high_part], 8, over_x)
+    far_to_x.wait_recv()
+    y_ref[low] += hop_ref[0]
+    y_low = send(y_ref.at[low], in_y_ref.at[low], 9, over_y)
+    own_in.wait_recv()
+    out_ref[...] = part_ref[me] + side_ref[3]
+    x_low.wait_recv()
+    out_ref[low] += in_x_ref[low]
+    y_high.wait_recv()
+    out_ref[high_part] += in_y_ref[high_part]
+    x_high.wait_recv()
+    out_ref[high_part] += in_x_ref[high_part]
+    y_low.wait_recv()
+    out_ref[low] += in_y_ref[low]
+    for copy in (far_in, x_in, y_in, own_in, far_to_x, far_to_y, x_low, y_high, x_high, y_low):
+        copy.wait_send()
+
+
+def scatter_blocks(parts, collective_id, name):
+    count = lax.axis_size("blk")
+    if count != 8 or parts.shape[1] % 2:
+        return lax.psum_scatter(parts, "blk", scatter_dimension=0, tiled=False)
+    shape = parts.shape[1:]
+    block = pltpu.VMEM(shape, parts.dtype)
+    return pl.pallas_call(
+        scatter_kernel,
+        in_specs=[pl.BlockSpec(memory_space=pltpu.VMEM)],
+        out_specs=pl.BlockSpec(memory_space=pltpu.VMEM),
+        out_shape=jax.ShapeDtypeStruct(shape, parts.dtype),
+        scratch_shapes=[
+            pltpu.VMEM((4,) + shape, parts.dtype),
+            block,
+            block,
+            block,
+            pltpu.VMEM((2, shape[0] // 2) + shape[1:], parts.dtype),
+            block,
+            block,
+            pltpu.SemaphoreType.DMA((10,)),
+            pltpu.SemaphoreType.DMA((10,)),
+        ],
+        compiler_params=pltpu.CompilerParams(
+            collective_id=collective_id, has_side_effects=True, vmem_limit_bytes=40 * 1024 * 1024
+        ),
+        cost_estimate=pl.CostEstimate(flops=0, bytes_accessed=2**26, transcendentals=0),
+        name=name,
+    )(parts)
+
+
+def collect_pairs(ids_ref, list_ref, mb_dev, block_count):
     me = lax.axis_index("blk")
     low = me * mb_dev
+    per_dev = block_count * R
 
     def scan(i, count):
         list_ref[count] = i
-        ident = ids_ref[i]
+        ident = ids_ref[i // per_dev, 0, i % per_dev]
         mine = (ident >= low) & (ident < low + mb_dev)
         return count + mine.astype(jnp.int32)
 
-    return lax.fori_loop(0, ids_ref.shape[0], scan, jnp.int32(0)), low
+    return lax.fori_loop(0, ids_ref.shape[0] * per_dev, scan, jnp.int32(0)), low
 
 
 def place(ids_ref, list_ref, low, block_count, i):
     at = list_ref[i]
-    block = at // R
-    return block // block_count, (block % block_count) * TB, (ids_ref[at] - low) * TB, block % block_count
+    dev = at // (block_count * R)
+    slot = at % (block_count * R)
+    sub = slot // R
+    return dev, sub * TB, (ids_ref[dev, 0, slot] - low) * TB, sub
 
 
 def far_forward(heads, mb_dev, block_count, scale, ids_ref, q_ref, k_ref, v_ref, out_ref, list_ref):
     out_ref[...] = jnp.zeros_like(out_ref)
-    count, low = collect_pairs(ids_ref, list_ref, mb_dev)
+    count, low = collect_pairs(ids_ref, list_ref, mb_dev, block_count)
     rows = q_ref.shape[2]
     ones = jnp.ones((8, 2 * TB), bf16)
 
@@ -93,7 +287,7 @@
     dq_ref[...] = jnp.zeros_like(dq_ref)
     dk_ref[...] = jnp.zeros_like(dk_ref)
     dv_ref[...] = jnp.zeros_like(dv_ref)
-    count, low = collect_pairs(ids_ref, list_ref, mb_dev)
+    count, low = collect_pairs(ids_ref, list_ref, mb_dev, block_count)
     rows = q_ref.shape[2]
 
     def step(i, carry):
@@ -148,9 +342,10 @@
     mb_dev = mem_rows // TB
     gate_mix = jax.nn.sigmoid(gate_bias)[:, None, None]
     hb = 2 if heads_dev % 2 == 0 else 1
-    ids_all = lax.all_gather(block_ids.reshape(-1), "blk", axis=0, tiled=True)
-    all_queries = lax.all_gather(queries, "blk", axis=0)
     prev_keys, prev_values = from_behind((key_rows, value_rows), "blk", 1)
+    flat_ids = block_ids.reshape(1, -1)
+    flat_ids = jnp.pad(flat_ids, ((0, 0), (0, -flat_ids.shape[1] % 128)))
+    all_queries, ids_all = gather_blocks(queries, 1, flat_ids)
 
     smem = pl.BlockSpec(memory_space=pltpu.SMEM)
     grid = (heads_dev // hb,)
@@ -158,7 +353,7 @@
     x_spec = pl.BlockSpec((blk_count, hb, shard_rows + EXTRA, head_width), lambda i: (0, i, 0, 0))
     m_spec = pl.BlockSpec((hb, mem_rows, head_width), lambda i: (i, 0, 0))
     params = pltpu.CompilerParams(vmem_limit_bytes=56 * 1024 * 1024)
-    scratch = [pltpu.SMEM((ids_all.shape[0] + 1,), jnp.int32)]
+    scratch = [pltpu.SMEM((blk_count * block_count * R + 1,), jnp.int32)]
     tile_flops = 2 * TB * TB * head_width * heads_dev * block_count * R
     partial = pl.pallas_call(
         functools.partial(far_forward, hb, mb_dev, block_count, score_scale),
@@ -191,7 +386,7 @@
     near_weights = near_exp / near_total
     local_out = jnp.einsum("hqk,hkd->hqd", near_weights, near_values, precision=high)
 
-    whole = lax.psum_scatter(partial, "blk", scatter_dimension=0, tiled=False)
+    whole = scatter_blocks(partial, 2, "scatter_out")
     far_total = whole[:, shard_rows : shard_rows + block_count].reshape(heads_dev, shard_rows, 1)
     memory_out = whole[:, :shard_rows] / far_total
 
@@ -227,7 +422,7 @@
         ],
         1,
     )
-    all_grad = lax.all_gather(jnp.concatenate([far_grad, tail], 1), "blk", axis=0)
+    all_grad = gather_blocks(jnp.concatenate([far_grad, tail], 1), 3)
     dq_all, memory_key_grad, memory_value_grad = pl.pallas_call(
         functools.partial(far_backward, hb, mb_dev, block_count, score_scale),
         grid=grid,
@@ -245,7 +440,7 @@
         ),
         name="far_backward",
     )(ids_all, all_queries, all_grad, memory_keys, memory_values)
-    far_query_grad = lax.psum_scatter(dq_all, "blk", scatter_dimension=0, tiled=False) * score_scale
+    far_query_grad = scatter_blocks(dq_all, 4, "scatter_query_grad") * score_scale
 
     near_delta = jnp.sum(near_grad * local_out, -1, keepdims=True)
     near_dp = jnp.einsum("hqd,hkd->hqk", near_grad, near_values, precision=high)

time: 315 us -> 266 us (0.84)
  waiting for transfers between devices: 151 us -> 0.01 us
  Pallas kernels: 81.4 us -> 206 us
  between operations: 15.3 us -> 1.68 us
  blocking collectives: 17.5 us -> 9.95 us
  starting transfers between devices: 19.4 us -> 13.6 us
  local copies, waits for them, and re-layouts: 5.17 us -> 10.8 us
    pallas_call x0 -> x4, Pallas kernels: none -> 146 us  [the longest x2 86.1 us: scatter_blocks(): pl.pallas_call(scatter_kernel, in_specs=[pl.BlockSpec(memory_space=pltpu....]
    all_gather x2 -> x0, waiting for transfers between devices: 67.5 us -> none  [the longest x1 37 us: local(): lax.all_gather(jnp.concatenate([far_grad, tail], 1), 'blk', axis=0)]
    reduce_scatter x2 -> x0, waiting for transfers between devices: 66.5 us -> none  [the longest x1 33.5 us: local(): whole = lax.psum_scatter(partial, 'blk', scatter_dimension=0, tiled=False)]
    ppermute x4, waiting for transfers between devices: 16.1 us -> 0.01 us  [from_behind(): return lax.ppermute(x, axis, pairs)]
    pallas_call x1, Pallas kernels: 51 us -> 35.6 us  [local(): pl.pallas_call(functools.partial(far_backward, hb, mb_dev, block_count, s...]
    unnamed x1 -> x0, blocking collectives: 7.81 us -> none
    pallas_call x1, Pallas kernels: 30.4 us -> 23.9 us  [local(): pl.pallas_call(functools.partial(far_forward, hb, mb_dev, block_count, sc...]
    ppermute x4, starting transfers between devices: 19.3 us -> 13.6 us  [from_behind(): return lax.ppermute(x, axis, pairs)]
  transfers between devices with their start and end apart: 8 -> 4, of which waited for: 8 -> 0; matrix products, arithmetic and copies ran while one was open for 4% -> 4% of each run, Pallas kernels for 0% -> 78%
where the time goes in v2:
time: 266 us; the launch traced here: 264 us
  Pallas kernels  206 us (77%)
  matrix products  14.2 us (5%)
  starting transfers between devices  13.6 us (5%)
  local copies, waits for them, and re-layouts  10.8 us (4%)
  blocking collectives  9.95 us (4%)
  other arithmetic  7.8 us (3%)
    pallas_call x2, Pallas kernels, scatter_blocks(): pl.pallas_call(scatter_kernel, in_specs=[pl.BlockSpec(memory_space=pltpu....  86.1 us
    pallas_call x1, Pallas kernels, local(): pl.pallas_call(functools.partial(far_backward, hb, mb_dev, block_count, s...  35.6 us
    pallas_call x1, Pallas kernels, gather_blocks(): pl.pallas_call(gather_ids_kernel, in_specs=[any_space, pl.BlockSpec(memor...  30.8 us
    pallas_call x1, Pallas kernels, gather_blocks(): pl.pallas_call(gather_kernel, in_specs=[any_space], out_specs=any_space,...  29.3 us
    pallas_call x1, Pallas kernels, local(): pl.pallas_call(functools.partial(far_forward, hb, mb_dev, block_count, sc...  23.9 us
    ppermute x4, starting transfers between devices, from_behind(): return lax.ppermute(x, axis, pairs)  13.6 us
    psum x1, blocking collectives, local(): lax.psum(jnp.stack([jnp.sum(mixed * mixed, axis=(0, 2)), jnp.sum(scaled_g...  9.95 us
    unnamed x39, local copies, waits for them, and re-layouts  7.72 us
  transfers between devices with their start and end apart: 4, of which 0 were waited for; matrix products, arithmetic and copies ran while one was open for 4% of the time, Pallas kernels for 78%

profile of v2, /device:TPU:1, one launch (start us, length us, event | category | flops | bytes accessed | tf_op | source)
XLA Modules:
  0.0 263.8 jit_solution(3592688932398525471)
XLA Ops:
  0.6 4.5 %collective-permute-start = (f32[4,256,128]{2,1,0:T(8,128)}, f32[4,256,128]{2,1,0:T(8,128)}, u32[]{:S(2)}, u32[]{:S(2)}) collective-permute-start(f32[4,256,128]{2,1,0:T(8,128)} %param.11), channel_id=1, source_target_pairs={{0,4},{4,8},{8,12},{12,16},{16,20},{20,24},{24,28},{1,5},{5,9},{9,... | collective-permute-start | bytes 1572872 | tf_op jit(solution)/shard_map/ppermute | solution.py:26
  5.2 1.9 collective-permute-start.1
  7.1 0.8 reshape.106
  7.9 0.5 pad.4.ids_ref
  8.4 30.8 %gather_queries.1 = (f32[8,4,256,128]{3,2,1,0:T(8,128)}, s32[8,1,128]{2,1,0:T(1,128)}) custom-call(f32[4,256,128]{2,1,0:T(8,128)} %x_ref.1, s32[1,128]{1,0:T(1,128)} %pad.4.ids_ref), custom_call_target="tpu_custom_call" | custom-call | bytes 67108864 | tf_op jit(solution)/shard_map/gather_queries/pallas_call | solution.py:148
  39.2 23.9 %far_forward.1.part_ref = f32[8,4,264,128]{3,2,1,0:T(8,128)} custom-call(s32[8,1,128]{2,1,0:T(1,128)} %get-tuple-element.10.ids_ref, f32[8,4,256,128]{3,2,1,0:T(8,128)} %get-tuple-element.11.q_ref, bf16[4,2048,128]{2,1,0:T(8,128)(2,1)} %k_ref.3, bf16[4,2048,128]{2,1,0:T(8,128)(2,1)} %v_ref.3), custom_call_target="tpu_custom_call" | custom-call | flops 4294967296 | bytes 12582912 | tf_op jit(solution)/shard_map/far_forward/pallas_call | solution.py:358
  63.2 2.2 copy-done
  65.4 38.5 %scatter_out.1 = f32[4,264,128]{2,1,0:T(8,128)S(1)} custom-call(f32[8,4,264,128]{3,2,1,0:T(8,128)S(1)} %copy-done), custom_call_target="tpu_custom_call" | custom-call | bytes 67108864 | tf_op jit(solution)/shard_map/scatter_out/pallas_call | solution.py:215
  103.9 0.0 copy-start.13
  104.7 0.1 pad.8.clone
  104.7 0.2 fusion.7
  104.9 0.0 copy-start.2
  104.9 0.0 collective-permute-done
  104.9 1.1 constant_dynamic-update-slice_fusion.1
  106.1 0.0 copy-done.12
  106.1 0.0 collective-permute-done.1
  106.1 1.1 constant_dynamic-update-slice_fusion.3
  107.3 0.0 copy-start.15
  107.3 0.0 copy-start.14
  107.3 0.0 copy-start.16
  107.3 1.3 fusion.1
  108.7 0.0 copy-start.6
  108.7 0.0 copy-done.14
  108.7 0.0 copy-done.16
  108.7 3.1 %multiply_reduce_fusion.3 = (f32[256]{0:T(256)S(1)}, f32[256]{0:T(256)S(1)}, f32[4,256,128]{2,1,0:T(8,128)}, f32[4,256,128]{2,1,0:T(8,128)S(1)}) fusion(f32[4,256,128]{2,1,0:T(8,128)S(1)} %copy-done.14, s32[]{:T(128)} %bitcast.30, s32[4]{0:T(128)S(1)} %multiply_add_fusion.1, f32[4,128]{1,0:T(4,128)S(1)} %copy-done.16, f32[4,256]{1,0:T(4,128)S(1)} %bitcast.32, ...), kind=kOutput, calls=%fused_computation.20 | convolution fusion | flops 407633408 | bytes 5386292 | tf_op jit(solution)/shard_map/hqk,hkd->hqd/dot_general | solution.py:387
  111.9 9.9 %psum.7 = f32[2,256]{1,0:T(2,128)S(1)} all-reduce(f32[2,256]{1,0:T(2,128)S(1)} %pad_maximum_fusion), channel_id=1, replica_groups=mesh['blk'=8,'head'=4] {'head'}, use_global_device_ids=true, to_apply=%region_3.4 | all-reduce | flops 512 | bytes 4096 | tf_op jit(solution)/shard_map/psum | solution.py:404
  121.8 2.6 multiply_reduce_fusion
  124.4 2.3 fusion.8
  126.8 0.3 multiply_reduce_fusion.1
  127.1 0.0 copy-start.3
  127.1 3.7 %multiply_multiply_fusion = f32[4,256,512]{1,2,0:T(8,128)S(1)} fusion(f32[4,512,128]{2,1,0:T(8,128)} %copy-done.15, f32[4,256]{1,0:T(4,128)S(1)} %multiply_reduce_fusion.1, f32[4,256,128]{2,1,0:T(8,128)} %copy-done.9, f32[4]{0:T(128)S(1)} %get-tuple-element.22, f32[4,256]{1,0:T(4,128)S(1)} %get-tuple-element.27, f32[4,512,256]{2,1,0:T(8,128)} %copy-done.6, ...), kind=kOutput, calls=%fused_computation.1 | convolution fusion | flops 405929984 | bytes 5906448 | tf_op jit(solution)/shard_map/hqd,hkd->hqk/dot_general | solution.py:446
  130.8 0.8 slice.37
  131.7 5.1 %collective-permute-start.3 = (f32[4,256,128]{2,1,0:T(8,128)}, f32[4,256,128]{2,1,0:T(8,128)}, u32[]{:S(2)}, u32[]{:S(2)}) collective-permute-start(f32[4,256,128]{2,1,0:T(8,128)} %slice.37), channel_id=1, source_target_pairs={{4,0},{8,4},{12,8},{16,12},{20,16},{24,20},{28,24},{5,1},{9,5},{13... | collective-permute-start | bytes 1572872 | tf_op jit(solution)/shard_map/ppermute | solution.py:26
  136.8 0.0 copy-done.3
  136.8 1.0 fusion.18
  137.8 1.0 copy-done.4
  138.8 0.8 slice.35
  139.6 2.1 collective-permute-start.2
  141.7 0.9 maximum_maximum_fusion.x_ref
  142.6 29.3 %gather_grad.1.g_ref = f32[8,4,264,128]{3,2,1,0:T(8,128)} custom-call(f32[4,264,128]{2,1,0:T(8,128)} %maximum_maximum_fusion.x_ref), custom_call_target="tpu_custom_call" | custom-call | bytes 67108864 | tf_op jit(solution)/shard_map/gather_grad/pallas_call | solution.py:138
  172.0 35.6 %far_backward.1 = (f32[8,4,256,128]{3,2,1,0:T(8,128)}, f32[4,2048,128]{2,1,0:T(8,128)}, f32[4,2048,128]{2,1,0:T(8,128)}) custom-call(s32[8,1,128]{2,1,0:T(1,128)} %get-tuple-element.10.ids_ref, f32[8,4,256,128]{3,2,1,0:T(8,128)} %get-tuple-element.11.q_ref, f32[8,4,264,128]{3,2,1,0:T(8,128)} %gather_grad.1.g_ref, bf16[4,2048,128]{2,1,0:T(8,128)(2,1)} %k_ref.3, ...), custom_call_target="tpu_custom_call" | custom-call | flops 12884901888 | bytes 25165824 | tf_op jit(solution)/shard_map/far_backward/pallas_call | solution.py:426
  207.6 2.2 copy-done.1
  209.7 47.6 %scatter_query_grad.1 = f32[4,256,128]{2,1,0:T(8,128)S(1)} custom-call(f32[8,4,256,128]{3,2,1,0:T(8,128)S(1)} %copy-done.1), custom_call_target="tpu_custom_call" | custom-call | bytes 67108864 | tf_op jit(solution)/shard_map/scatter_query_grad/pallas_call | solution.py:215
  257.3 2.6 convolution_add_fusion
  260.0 0.0 collective-permute-done.3
  260.0 1.9 slice_add_fusion
  261.8 0.0 collective-permute-done.2
  261.9 1.9 slice_add_fusion.1
  (34 shorter events, 0.2 us)
Async XLA Ops:
  0.6 104.3 %collective-permute-start = (f32[4,256,128]{2,1,0:T(8,128)}, f32[4,256,128]{2,1,0:T(8,128)}, u32[]{:S(2)}, u32[]{:S(2)}) collective-permute-start(f32[4,256,128]{2,1,0:T(8,128)} %param.11), channel_id=1, source_target_pairs={{0,4},{4,8},{8,12},{12,16},{16,20},{20,24},{24,28},{1,5},{5,9},{9,... | collective-permute-start | bytes 1572872 | tf_op jit(solution)/shard_map/ppermute | solution.py:26
  5.2 101.0 %collective-permute-start.1 = (f32[4,256,128]{2,1,0:T(8,128)}, f32[4,256,128]{2,1,0:T(8,128)}, u32[]{:S(2)}, u32[]{:S(2)}) collective-permute-start(f32[4,256,128]{2,1,0:T(8,128)} %param.12), channel_id=1, source_target_pairs={{0,4},{4,8},{8,12},{12,16},{16,20},{20,24},{24,28},{1,5},{5,9},{9,... | collective-permute-start | bytes 1572872 | tf_op jit(solution)/shard_map/ppermute | solution.py:26
  63.2 2.2 copy-start
  65.4 38.5 %copy-start.17 = (f32[4]{0:T(128)S(1)}, f32[4]{0:T(128)}, u32[]{:S(2)}) copy-start(f32[4]{0:T(128)} %param.15) | copy-start | bytes 52
  65.4 40.7 %copy-start.12 = (f32[4,256,128]{2,1,0:T(8,128)S(1)}, f32[4,256,128]{2,1,0:T(8,128)}, u32[]{:S(2)}) copy-start(f32[4,256,128]{2,1,0:T(8,128)} %param.11) | copy-start | bytes 1572868
  103.9 3.3 %copy-start.13 = (f32[4,256,128]{2,1,0:T(8,128)S(1)}, f32[4,256,128]{2,1,0:T(8,128)}, u32[]{:S(2)}) copy-start(f32[4,256,128]{2,1,0:T(8,128)} %param.12) | copy-start | bytes 1572868
  104.9 2.4 copy-start.2
  107.3 4.6 %copy-start.15 = (f32[4,512,128]{2,1,0:T(8,128)}, f32[4,512,128]{2,1,0:T(8,128)S(1)}, u32[]{:S(2)}) copy-start(f32[4,512,128]{2,1,0:T(8,128)S(1)} %constant_dynamic-update-slice_fusion.2) | copy-start | bytes 3145732
  107.3 1.4 copy-start.14
  107.3 1.4 copy-start.16
  108.7 3.2 %copy-start.6 = (f32[4,512,256]{2,1,0:T(8,128)}, f32[4,512,256]{2,1,0:T(8,128)S(1)}, u32[]{:S(2)}) copy-start(f32[4,512,256]{2,1,0:T(8,128)S(1)} %get-tuple-element.28) | copy-start | bytes 6291460
  121.8 2.6 copy-start.7
  124.4 2.4 copy-start.9
  127.1 3.7 %copy-start.10 = (f32[4,512,128]{2,1,0:T(8,128)S(1)}, f32[4,512,128]{2,1,0:T(8,128)}, u32[]{:S(2)}) copy-start(f32[4,512,128]{2,1,0:T(8,128)} %fusion.8) | copy-start | bytes 3145732
  127.1 9.7 %copy-start.3 = (f32[4,256,128]{2,1,0:T(8,128)S(1)}, f32[4,256,128]{2,1,0:T(8,128)}, u32[]{:S(2)}) copy-start(f32[4,256,128]{2,1,0:T(8,128)} %x_ref.1) | copy-start | bytes 1572868
  131.7 10.1 %copy-start.8 = (f32[4,256,128]{2,1,0:T(8,128)S(1)}, f32[4,256,128]{2,1,0:T(8,128)}, u32[]{:S(2)}) copy-start(f32[4,256,128]{2,1,0:T(8,128)} %get-tuple-element.18) | copy-start | bytes 1572868
  131.7 128.3 %collective-permute-start.3 = (f32[4,256,128]{2,1,0:T(8,128)}, f32[4,256,128]{2,1,0:T(8,128)}, u32[]{:S(2)}, u32[]{:S(2)}) collective-permute-start(f32[4,256,128]{2,1,0:T(8,128)} %slice.37), channel_id=1, source_target_pairs={{4,0},{8,4},{12,8},{16,12},{20,16},{24,20},{28,24},{5,1},{9,5},{13... | collective-permute-start | bytes 1572872 | tf_op jit(solution)/shard_map/ppermute | solution.py:26
  137.8 1.0 copy-start.4
  139.6 122.2 %collective-permute-start.2 = (f32[4,256,128]{2,1,0:T(8,128)}, f32[4,256,128]{2,1,0:T(8,128)}, u32[]{:S(2)}, u32[]{:S(2)}) collective-permute-start(f32[4,256,128]{2,1,0:T(8,128)} %slice.35), channel_id=1, source_target_pairs={{4,0},{8,4},{12,8},{16,12},{20,16},{24,20},{28,24},{5,1},{9,5},{13... | collective-permute-start | bytes 1572872 | tf_op jit(solution)/shard_map/ppermute | solution.py:26
  207.6 2.2 copy-start.1
  257.3 2.6 copy-start.11
  257.3 4.5 %copy-start.5 = (f32[4,512,128]{2,1,0:T(8,128)S(1)}, f32[4,512,128]{2,1,0:T(8,128)}, u32[]{:S(2)}) copy-start(f32[4,512,128]{2,1,0:T(8,128)} %copy-done.4) | copy-start | bytes 3145732

commit v3 on v2

--- a/solution.py
+++ b/solution.py
@@ -236,31 +236,39 @@
     )(parts)
 
 
-def collect_pairs(ids_ref, list_ref, mb_dev, block_count):
+def collect_pairs(ids_ref, list_ref, mb_dev):
     me = lax.axis_index("blk")
     low = me * mb_dev
-    per_dev = block_count * R
-
-    def scan(i, count):
-        list_ref[count] = i
-        ident = ids_ref[i // per_dev, 0, i % per_dev]
-        mine = (ident >= low) & (ident < low + mb_dev)
-        return count + mine.astype(jnp.int32)
-
-    return lax.fori_loop(0, ids_ref.shape[0] * per_dev, scan, jnp.int32(0)), low
+    total = ids_ref.shape[0]
+
+    @pl.when(pl.program_id(0) == 0)
+    def _():
+        def scan(i, count):
+            for j in range(8):
+                at = i * 8 + j
+                list_ref[count] = at
+                ident = ids_ref[at]
+                mine = (ident >= low) & (ident < low + mb_dev)
+                count = count + mine.astype(jnp.int32)
+            return count
+
+        count = lax.fori_loop(0, total // 8, scan, jnp.int32(0))
+        list_ref[total + 1] = count
+
+    return list_ref[total + 1], low
 
 
 def place(ids_ref, list_ref, low, block_count, i):
     at = list_ref[i]
-    dev = at // (block_count * R)
-    slot = at % (block_count * R)
-    sub = slot // R
-    return dev, sub * TB, (ids_ref[dev, 0, slot] - low) * TB, sub
+    block = lax.div(at, jnp.int32(R))
+    dev = lax.div(block, jnp.int32(block_count))
+    sub = block - dev * block_count
+    return dev, sub * TB, (ids_ref[at] - low) * TB, sub
 
 
 def far_forward(heads, mb_dev, block_count, scale, ids_ref, q_ref, k_ref, v_ref, out_ref, list_ref):
     out_ref[...] = jnp.zeros_like(out_ref)
-    count, low = collect_pairs(ids_ref, list_ref, mb_dev, block_count)
+    count, low = collect_pairs(ids_ref, list_ref, mb_dev)
     rows = q_ref.shape[2]
     ones = jnp.ones((8, 2 * TB), bf16)
 
@@ -287,7 +295,7 @@
     dq_ref[...] = jnp.zeros_like(dq_ref)
     dk_ref[...] = jnp.zeros_like(dk_ref)
     dv_ref[...] = jnp.zeros_like(dv_ref)
-    count, low = collect_pairs(ids_ref, list_ref, mb_dev, block_count)
+    count, low = collect_pairs(ids_ref, list_ref, mb_dev)
     rows = q_ref.shape[2]
 
     def step(i, carry):
@@ -346,6 +354,7 @@
     flat_ids = block_ids.reshape(1, -1)
     flat_ids = jnp.pad(flat_ids, ((0, 0), (0, -flat_ids.shape[1] % 128)))
     all_queries, ids_all = gather_blocks(queries, 1, flat_ids)
+    ids_all = ids_all[:, 0, : block_count * R].reshape(-1)
 
     smem = pl.BlockSpec(memory_space=pltpu.SMEM)
     grid = (heads_dev // hb,)
@@ -353,7 +362,7 @@
     x_spec = pl.BlockSpec((blk_count, hb, shard_rows + EXTRA, head_width), lambda i: (0, i, 0, 0))
     m_spec = pl.BlockSpec((hb, mem_rows, head_width), lambda i: (i, 0, 0))
     params = pltpu.CompilerParams(vmem_limit_bytes=56 * 1024 * 1024)
-    scratch = [pltpu.SMEM((blk_count * block_count * R + 1,), jnp.int32)]
+    scratch = [pltpu.SMEM((blk_count * block_count * R + 2,), jnp.int32)]
     tile_flops = 2 * TB * TB * head_width * heads_dev * block_count * R
     partial = pl.pallas_call(
         functools.partial(far_forward, hb, mb_dev, block_count, score_scale),

time: 266 us -> 253 us (0.951)
  Pallas kernels: 206 us -> 193 us
    pallas_call x2, Pallas kernels: 86.1 us -> 47.2 us  [scatter_blocks(): pl.pallas_call(scatter_kernel, in_specs=[pl.BlockSpec(memory_space=pltpu....]
    pallas_call x1, Pallas kernels: 35.6 us -> 53 us  [local(): pl.pallas_call(functools.partial(far_backward, hb, mb_dev, block_count, s...]
    pallas_call x1, Pallas kernels: 23.9 us -> 30.4 us  [local(): pl.pallas_call(functools.partial(far_forward, hb, mb_dev, block_count, sc...]
  transfers between devices with their start and end apart: 4 -> 4, of which waited for: 0 -> 0; matrix products, arithmetic and copies ran while one was open for 4% -> 4% of each run, Pallas kernels for 78% -> 77%
where the time goes in v3:
time: 253 us; the launch traced here: 251 us
  Pallas kernels  193 us (76%)
  matrix products  14.2 us (6%)
  starting transfers between devices  12.2 us (5%)
  local copies, waits for them, and re-layouts  12.1 us (5%)
  blocking collectives  9.96 us (4%)
  other arithmetic  7.8 us (3%)
    pallas_call x1, Pallas kernels, local(): pl.pallas_call(functools.partial(far_backward, hb, mb_dev, block_count, s...  53 us
    pallas_call x2, Pallas kernels, scatter_blocks(): pl.pallas_call(scatter_kernel, in_specs=[pl.BlockSpec(memory_space=pltpu....  47.2 us
    pallas_call x1, Pallas kernels, gather_blocks(): pl.pallas_call(gather_kernel, in_specs=[any_space], out_specs=any_space,...  31.9 us
    pallas_call x1, Pallas kernels, gather_blocks(): pl.pallas_call(gather_ids_kernel, in_specs=[any_space, pl.BlockSpec(memor...  30.8 us
    pallas_call x1, Pallas kernels, local(): pl.pallas_call(functools.partial(far_forward, hb, mb_dev, block_count, sc...  30.4 us
    ppermute x4, starting transfers between devices, from_behind(): return lax.ppermute(x, axis, pairs)  12.2 us
    psum x1, blocking collectives, local(): lax.psum(jnp.stack([jnp.sum(mixed * mixed, axis=(0, 2)), jnp.sum(scaled_g...  9.96 us
    unnamed x39, local copies, waits for them, and re-layouts  7.68 us
  transfers between devices with their start and end apart: 4, of which 0 were waited for; matrix products, arithmetic and copies ran while one was open for 4% of the time, Pallas kernels for 77%

profile of v3, /device:TPU:1, one launch (start us, length us, event | category | flops | bytes accessed | tf_op | source)
XLA Modules:
  0.0 251.3 jit_solution(13780831708480485568)
XLA Ops:
  0.6 4.5 %collective-permute-start = (f32[4,256,128]{2,1,0:T(8,128)}, f32[4,256,128]{2,1,0:T(8,128)}, u32[]{:S(2)}, u32[]{:S(2)}) collective-permute-start(f32[4,256,128]{2,1,0:T(8,128)} %param.11), channel_id=1, source_target_pairs={{0,4},{4,8},{8,12},{12,16},{16,20},{20,24},{24,28},{1,5},{5,9},{9,... | collective-permute-start | bytes 1572872 | tf_op jit(solution)/shard_map/ppermute | solution.py:26
  5.2 1.9 collective-permute-start.1
  7.1 0.8 reshape.106
  7.9 0.5 pad.4.ids_ref
  8.4 30.8 %gather_queries.1 = (f32[8,4,256,128]{3,2,1,0:T(8,128)}, s32[8,1,128]{2,1,0:T(1,128)}) custom-call(f32[4,256,128]{2,1,0:T(8,128)} %x_ref.1, s32[1,128]{1,0:T(1,128)} %pad.4.ids_ref), custom_call_target="tpu_custom_call" | custom-call | bytes 67108864 | tf_op jit(solution)/shard_map/gather_queries/pallas_call | solution.py:148
  39.3 0.7 slice_reduce_fusion
  39.9 0.6 reshape_squeeze.3.ids_ref
  40.6 30.4 %far_forward.1.part_ref = f32[8,4,264,128]{3,2,1,0:T(8,128)} custom-call(s32[256]{0:T(256)} %reshape_squeeze.3.ids_ref, f32[8,4,256,128]{3,2,1,0:T(8,128)} %get-tuple-element.11.q_ref, bf16[4,2048,128]{2,1,0:T(8,128)(2,1)} %k_ref.3, bf16[4,2048,128]{2,1,0:T(8,128)(2,1)} %v_ref.3), custom_call_target="tpu_custom_call" | custom-call | flops 4294967296 | bytes 12582912 | tf_op jit(solution)/shard_map/far_forward/pallas_call | solution.py:367
  71.0 2.2 copy-done
  73.2 24.1 %scatter_out.1 = f32[4,264,128]{2,1,0:T(8,128)S(1)} custom-call(f32[8,4,264,128]{3,2,1,0:T(8,128)S(1)} %copy-done), custom_call_target="tpu_custom_call" | custom-call | bytes 67108864 | tf_op jit(solution)/shard_map/scatter_out/pallas_call | solution.py:215
  97.4 0.0 copy-start.13
  98.1 0.1 pad.8.clone
  98.2 0.2 fusion.7
  98.4 0.0 copy-start.2
  98.4 0.0 collective-permute-done
  98.4 1.1 constant_dynamic-update-slice_fusion.1
  99.6 0.0 collective-permute-done.1
  99.6 1.1 constant_dynamic-update-slice_fusion.3
  100.7 0.0 copy-done.2
  100.7 0.0 copy-start.15
  100.8 0.0 copy-start.14
  100.8 0.0 copy-start.16
  100.8 1.3 fusion.1
  102.1 0.0 copy-start.6
  102.1 0.0 copy-done.14
  102.2 3.1 %multiply_reduce_fusion.3 = (f32[256]{0:T(256)S(1)}, f32[256]{0:T(256)S(1)}, f32[4,256,128]{2,1,0:T(8,128)}, f32[4,256,128]{2,1,0:T(8,128)S(1)}) fusion(f32[4,256,128]{2,1,0:T(8,128)S(1)} %copy-done.14, s32[]{:T(128)} %bitcast.30, s32[4]{0:T(128)S(1)} %multiply_add_fusion.1, f32[4,128]{1,0:T(4,128)S(1)} %copy-done.16, f32[4,256]{1,0:T(4,128)S(1)} %bitcast.32, ...), kind=kOutput, calls=%fused_computation.20 | convolution fusion | flops 407633408 | bytes 5386292 | tf_op jit(solution)/shard_map/hqk,hkd->hqd/dot_general | solution.py:396
  105.3 10.0 %psum.7 = f32[2,256]{1,0:T(2,128)S(1)} all-reduce(f32[2,256]{1,0:T(2,128)S(1)} %pad_maximum_fusion), channel_id=1, replica_groups=mesh['blk'=8,'head'=4] {'head'}, use_global_device_ids=true, to_apply=%region_3.4 | all-reduce | flops 512 | bytes 4096 | tf_op jit(solution)/shard_map/psum | solution.py:413
  115.3 2.6 %multiply_reduce_fusion = (f32[4,256]{1,0:T(4,128)S(1)}, f32[4,256,128]{2,1,0:T(8,128)}, f32[4,256,128]{2,1,0:T(8,128)S(1)}) fusion(f32[4,256]{1,0:T(4,128)S(1)} %bitcast.33, f32[4,264,128]{2,1,0:T(8,128)S(1)} %scatter_out.1, f32[4]{0:T(128)S(1)} %get-tuple-element.21, f32[256]{0:T(256)S(1)} %bitcast.35, f32[4,256,128]{2,1,0:T(8,128)} %get-tuple-element.20, ...), kind=kLoop, calls=%fused_computation.15 | loop fusion | flops 3668992 | bytes 2633764 | tf_op jit(solution)/shard_map/reduce_sum | solution.py:425
  117.9 2.4 fusion.8
  120.3 0.3 multiply_reduce_fusion.1
  120.6 0.0 copy-start.3
  120.6 3.7 %multiply_multiply_fusion = f32[4,256,512]{1,2,0:T(8,128)S(1)} fusion(f32[4,512,128]{2,1,0:T(8,128)} %copy-done.15, f32[4,256]{1,0:T(4,128)S(1)} %multiply_reduce_fusion.1, f32[4,256,128]{2,1,0:T(8,128)} %copy-done.9, f32[4]{0:T(128)S(1)} %get-tuple-element.22, f32[4,256]{1,0:T(4,128)S(1)} %get-tuple-element.27, f32[4,512,256]{2,1,0:T(8,128)} %copy-done.6, ...), kind=kOutput, calls=%fused_computation.1 | convolution fusion | flops 405929984 | bytes 5906448 | tf_op jit(solution)/shard_map/hqd,hkd->hqk/dot_general | solution.py:455
  124.3 0.9 slice.41
  125.2 3.7 %collective-permute-start.3 = (f32[4,256,128]{2,1,0:T(8,128)}, f32[4,256,128]{2,1,0:T(8,128)}, u32[]{:S(2)}, u32[]{:S(2)}) collective-permute-start(f32[4,256,128]{2,1,0:T(8,128)} %slice.41), channel_id=1, source_target_pairs={{4,0},{8,4},{12,8},{16,12},{20,16},{24,20},{28,24},{5,1},{9,5},{13... | collective-permute-start | bytes 1572872 | tf_op jit(solution)/shard_map/ppermute | solution.py:26
  128.9 1.0 fusion.18
  129.9 0.9 copy-done.4
  130.9 0.8 slice.39
  131.7 2.1 collective-permute-start.2
  133.8 0.9 maximum_maximum_fusion.x_ref
  134.7 31.9 %gather_grad.1.g_ref = f32[8,4,264,128]{3,2,1,0:T(8,128)} custom-call(f32[4,264,128]{2,1,0:T(8,128)} %maximum_maximum_fusion.x_ref), custom_call_target="tpu_custom_call" | custom-call | bytes 67108864 | tf_op jit(solution)/shard_map/gather_grad/pallas_call | solution.py:138
  166.6 53.0 %far_backward.1 = (f32[8,4,256,128]{3,2,1,0:T(8,128)}, f32[4,2048,128]{2,1,0:T(8,128)}, f32[4,2048,128]{2,1,0:T(8,128)}) custom-call(s32[256]{0:T(256)} %reshape_squeeze.3.ids_ref, f32[8,4,256,128]{3,2,1,0:T(8,128)} %get-tuple-element.11.q_ref, f32[8,4,264,128]{3,2,1,0:T(8,128)} %gather_grad.1.g_ref, bf16[4,2048,128]{2,1,0:T(8,128)(2,1)} %k_ref.3, ...), custom_call_target="tpu_custom_call" | custom-call | flops 12884901888 | bytes 25165824 | tf_op jit(solution)/shard_map/far_backward/pallas_call | solution.py:435
  219.6 2.2 copy-done.1
  221.8 23.1 %scatter_query_grad.1 = f32[4,256,128]{2,1,0:T(8,128)S(1)} custom-call(f32[8,4,256,128]{3,2,1,0:T(8,128)S(1)} %copy-done.1), custom_call_target="tpu_custom_call" | custom-call | bytes 67108864 | tf_op jit(solution)/shard_map/scatter_query_grad/pallas_call | solution.py:215
  244.9 2.6 %convolution_add_fusion = f32[4,256,128]{2,1,0:T(8,128)} fusion(f32[4,256,512]{1,2,0:T(8,128)S(1)} %multiply_multiply_fusion, f32[4,512,128]{2,1,0:T(8,128)S(1)} %constant_dynamic-update-slice_fusion, f32[4,256,128]{2,1,0:T(8,128)S(1)} %scatter_query_grad.1), kind=kOutput, calls=%fused_computation.4 | convolution fusion | flops 402915328 | bytes 4194304 | tf_op jit(solution)/shard_map/hqk,hkd->hqd/dot_general | solution.py:464
  247.5 0.0 collective-permute-done.3
  247.5 1.9 slice_add_fusion
  249.4 0.0 collective-permute-done.2
  249.4 1.9 slice_add_fusion.1
  (36 shorter events, 0.2 us)
Async XLA Ops:
  0.6 97.8 %collective-permute-start = (f32[4,256,128]{2,1,0:T(8,128)}, f32[4,256,128]{2,1,0:T(8,128)}, u32[]{:S(2)}, u32[]{:S(2)}) collective-permute-start(f32[4,256,128]{2,1,0:T(8,128)} %param.11), channel_id=1, source_target_pairs={{0,4},{4,8},{8,12},{12,16},{16,20},{20,24},{24,28},{1,5},{5,9},{9,... | collective-permute-start | bytes 1572872 | tf_op jit(solution)/shard_map/ppermute | solution.py:26
  5.2 94.4 %collective-permute-start.1 = (f32[4,256,128]{2,1,0:T(8,128)}, f32[4,256,128]{2,1,0:T(8,128)}, u32[]{:S(2)}, u32[]{:S(2)}) collective-permute-start(f32[4,256,128]{2,1,0:T(8,128)} %param.12), channel_id=1, source_target_pairs={{0,4},{4,8},{8,12},{12,16},{16,20},{20,24},{24,28},{1,5},{5,9},{9,... | collective-permute-start | bytes 1572872 | tf_op jit(solution)/shard_map/ppermute | solution.py:26
  71.0 2.2 copy-start
  73.2 24.2 %copy-start.17 = (f32[4]{0:T(128)S(1)}, f32[4]{0:T(128)}, u32[]{:S(2)}) copy-start(f32[4]{0:T(128)} %param.15) | copy-start | bytes 52
  73.2 26.3 %copy-start.12 = (f32[4,256,128]{2,1,0:T(8,128)S(1)}, f32[4,256,128]{2,1,0:T(8,128)}, u32[]{:S(2)}) copy-start(f32[4,256,128]{2,1,0:T(8,128)} %param.11) | copy-start | bytes 1572868
  97.4 3.3 %copy-start.13 = (f32[4,256,128]{2,1,0:T(8,128)S(1)}, f32[4,256,128]{2,1,0:T(8,128)}, u32[]{:S(2)}) copy-start(f32[4,256,128]{2,1,0:T(8,128)} %param.12) | copy-start | bytes 1572868
  98.4 2.4 copy-start.2
  100.7 4.6 %copy-start.15 = (f32[4,512,128]{2,1,0:T(8,128)}, f32[4,512,128]{2,1,0:T(8,128)S(1)}, u32[]{:S(2)}) copy-start(f32[4,512,128]{2,1,0:T(8,128)S(1)} %constant_dynamic-update-slice_fusion.2) | copy-start | bytes 3145732
  100.8 1.4 copy-start.14
  100.8 1.4 copy-start.16
  102.1 3.2 %copy-start.6 = (f32[4,512,256]{2,1,0:T(8,128)}, f32[4,512,256]{2,1,0:T(8,128)S(1)}, u32[]{:S(2)}) copy-start(f32[4,512,256]{2,1,0:T(8,128)S(1)} %get-tuple-element.28) | copy-start | bytes 6291460
  115.3 2.6 %copy-start.7 = (f32[4,512,256]{2,1,0:T(8,128)S(1)}, f32[4,512,256]{2,1,0:T(8,128)}, u32[]{:S(2)}) copy-start(f32[4,512,256]{2,1,0:T(8,128)} %copy-done.6) | copy-start | bytes 6291460
  117.9 2.4 copy-start.9
  120.6 3.7 %copy-start.10 = (f32[4,512,128]{2,1,0:T(8,128)S(1)}, f32[4,512,128]{2,1,0:T(8,128)}, u32[]{:S(2)}) copy-start(f32[4,512,128]{2,1,0:T(8,128)} %fusion.8) | copy-start | bytes 3145732
  120.6 8.3 %copy-start.3 = (f32[4,256,128]{2,1,0:T(8,128)S(1)}, f32[4,256,128]{2,1,0:T(8,128)}, u32[]{:S(2)}) copy-start(f32[4,256,128]{2,1,0:T(8,128)} %x_ref.1) | copy-start | bytes 1572868
  125.2 8.6 %copy-start.8 = (f32[4,256,128]{2,1,0:T(8,128)S(1)}, f32[4,256,128]{2,1,0:T(8,128)}, u32[]{:S(2)}) copy-start(f32[4,256,128]{2,1,0:T(8,128)} %get-tuple-element.18) | copy-start | bytes 1572868
  125.2 122.3 %collective-permute-start.3 = (f32[4,256,128]{2,1,0:T(8,128)}, f32[4,256,128]{2,1,0:T(8,128)}, u32[]{:S(2)}, u32[]{:S(2)}) collective-permute-start(f32[4,256,128]{2,1,0:T(8,128)} %slice.41), channel_id=1, source_target_pairs={{4,0},{8,4},{12,8},{16,12},{20,16},{24,20},{28,24},{5,1},{9,5},{13... | collective-permute-start | bytes 1572872 | tf_op jit(solution)/shard_map/ppermute | solution.py:26
  129.9 1.0 copy-start.4
  131.7 117.7 %collective-permute-start.2 = (f32[4,256,128]{2,1,0:T(8,128)}, f32[4,256,128]{2,1,0:T(8,128)}, u32[]{:S(2)}, u32[]{:S(2)}) collective-permute-start(f32[4,256,128]{2,1,0:T(8,128)} %slice.39), channel_id=1, source_target_pairs={{4,0},{8,4},{12,8},{16,12},{20,16},{24,20},{28,24},{5,1},{9,5},{13... | collective-permute-start | bytes 1572872 | tf_op jit(solution)/shard_map/ppermute | solution.py:26
  219.6 2.2 copy-start.1
  244.9 2.6 %copy-start.11 = (f32[4,512,128]{2,1,0:T(8,128)S(1)}, f32[4,512,128]{2,1,0:T(8,128)}, u32[]{:S(2)}) copy-start(f32[4,512,128]{2,1,0:T(8,128)} %fusion.8) | copy-start | bytes 3145732
  244.9 4.5 %copy-start.5 = (f32[4,512,128]{2,1,0:T(8,128)S(1)}, f32[4,512,128]{2,1,0:T(8,128)}, u32[]{:S(2)}) copy-start(f32[4,512,128]{2,1,0:T(8,128)} %copy-done.4) | copy-start | bytes 3145732

commit v4 on v3

--- a/solution.py
+++ b/solution.py
@@ -276,14 +276,17 @@
         dev, q_at, k_at, sub = place(ids_ref, list_ref, low, block_count, i)
         q_rows = pl.ds(pl.multiple_of(q_at, TB), TB)
         k_rows = pl.ds(pl.multiple_of(k_at, TB), TB)
-        for h in range(heads):
-            q2 = jnp.concatenate(split(q_ref[dev, h, q_rows, :] * scale), 1)
-            k = k_ref[h, k_rows, :]
-            v = v_ref[h, k_rows, :]
-            e = jnp.exp(dot(q2, jnp.concatenate([k, k], 1), 1, 1))
-            e2 = jnp.concatenate(split(e), 1)
-            out_ref[dev, h, q_rows, :] += dot(e2, jnp.concatenate([v, v], 0), 1, 0)
-            out_ref[dev, h, pl.ds(rows + sub, 1), :] += dot(ones, e2, 1, 1)[:1]
+        hs = range(heads)
+        twice = [jnp.concatenate(split(q_ref[dev, h, q_rows, :] * scale), 1) for h in hs]
+        ks = [k_ref[h, k_rows, :] for h in hs]
+        vs = [v_ref[h, k_rows, :] for h in hs]
+        scores = [dot(twice[h], jnp.concatenate([ks[h], ks[h]], 1), 1, 1) for h in hs]
+        e2 = [jnp.concatenate(split(jnp.exp(scores[h])), 1) for h in hs]
+        sums = [dot(e2[h], jnp.concatenate([vs[h], vs[h]], 0), 1, 0) for h in hs]
+        totals = [dot(ones, e2[h], 1, 1)[:1] for h in hs]
+        for h in hs:
+            out_ref[dev, h, q_rows, :] += sums[h]
+            out_ref[dev, h, pl.ds(rows + sub, 1), :] += totals[h]
         return carry
 
     lax.fori_loop(0, count, step, 0)
@@ -302,28 +305,33 @@
         dev, q_at, k_at, sub = place(ids_ref, list_ref, low, block_count, i)
         q_rows = pl.ds(pl.multiple_of(q_at, TB), TB)
         k_rows = pl.ds(pl.multiple_of(k_at, TB), TB)
-        for h in range(heads):
-            qh, ql = split(q_ref[dev, h, q_rows, :] * scale)
-            gh, gl = split(g_ref[dev, h, q_rows, :])
-            delta = g_ref[dev, h, pl.ds(rows + sub, 1), :]
-            rden = g_ref[dev, h, pl.ds(rows + block_count + sub, 1), :]
-            k = k_ref[h, k_rows, :]
-            v = v_ref[h, k_rows, :]
-            st = dot(jnp.concatenate([k, k], 1), jnp.concatenate([qh, ql], 1), 1, 1)
-            dp = dot(jnp.concatenate([v, v], 1), jnp.concatenate([gh, gl], 1), 1, 1)
-            p = jnp.exp(st) * rden
-            ds = p * (dp - delta)
-            ph, plo = split(p)
-            dh, dl = split(ds)
-            dk_ref[h, k_rows, :] += dot(
-                jnp.concatenate([dh, dl, dh], 1), jnp.concatenate([qh, qh, ql], 0), 1, 0
+        hs = range(heads)
+        q = [split(q_ref[dev, h, q_rows, :] * scale) for h in hs]
+        g = [split(g_ref[dev, h, q_rows, :]) for h in hs]
+        delta = [g_ref[dev, h, pl.ds(rows + sub, 1), :] for h in hs]
+        rden = [g_ref[dev, h, pl.ds(rows + block_count + sub, 1), :] for h in hs]
+        ks = [k_ref[h, k_rows, :] for h in hs]
+        vs = [v_ref[h, k_rows, :] for h in hs]
+        st = [dot(jnp.concatenate([ks[h], ks[h]], 1), jnp.concatenate(q[h], 1), 1, 1) for h in hs]
+        dp = [dot(jnp.concatenate([vs[h], vs[h]], 1), jnp.concatenate(g[h], 1), 1, 1) for h in hs]
+        weights = [jnp.exp(st[h]) * rden[h] for h in hs]
+        ds = [split(weights[h] * (dp[h] - delta[h])) for h in hs]
+        ps = [split(weights[h]) for h in hs]
+
+        def three(x, y):
+            return dot(
+                jnp.concatenate([x[0], x[1], x[0]], 1), jnp.concatenate([y[0], y[0], y[1]], 0), 1, 0
             )
-            dv_ref[h, k_rows, :] += dot(
-                jnp.concatenate([ph, plo, ph], 1), jnp.concatenate([gh, gh, gl], 0), 1, 0
-            )
-            dq_ref[dev, h, q_rows, :] += dot(
-                jnp.concatenate([dh, dl], 0), jnp.concatenate([k, k], 0), 0, 0
-            )
+
+        dv = [three(ps[h], g[h]) for h in hs]
+        dk = [three(ds[h], q[h]) for h in hs]
+        dq = [
+            dot(jnp.concatenate(ds[h], 0), jnp.concatenate([ks[h], ks[h]], 0), 0, 0) for h in hs
+        ]
+        for h in hs:
+            dv_ref[h, k_rows, :] += dv[h]
+            dk_ref[h, k_rows, :] += dk[h]
+            dq_ref[dev, h, q_rows, :] += dq[h]
         return carry
 
     lax.fori_loop(0, count, step, 0)

time: 253 us -> 238 us (0.941)
  Pallas kernels: 193 us -> 179 us
    pallas_call x1, Pallas kernels: 53 us -> 40.6 us  [local(): pl.pallas_call(functools.partial(far_backward, hb, mb_dev, block_count, s...]
  transfers between devices with their start and end apart: 4 -> 4, of which waited for: 0 -> 0; matrix products, arithmetic and copies ran while one was open for 4% -> 5% of each run, Pallas kernels for 77% -> 76%
where the time goes in v4:
time: 238 us; the launch traced here: 237 us
  Pallas kernels  179 us (75%)
  matrix products  14.2 us (6%)
  local copies, waits for them, and re-layouts  12.1 us (5%)
  starting transfers between devices  11.8 us (5%)
  blocking collectives  10.3 us (4%)
  other arithmetic  7.8 us (3%)
    pallas_call x2, Pallas kernels, scatter_blocks(): pl.pallas_call(scatter_kernel, in_specs=[pl.BlockSpec(memory_space=pltpu....  45.7 us
    pallas_call x1, Pallas kernels, local(): pl.pallas_call(functools.partial(far_backward, hb, mb_dev, block_count, s...  40.6 us
    pallas_call x1, Pallas kernels, gather_blocks(): pl.pallas_call(gather_kernel, in_specs=[any_space], out_specs=any_space,...  31.7 us
    pallas_call x1, Pallas kernels, gather_blocks(): pl.pallas_call(gather_ids_kernel, in_specs=[any_space, pl.BlockSpec(memor...  30.8 us
    pallas_call x1, Pallas kernels, local(): pl.pallas_call(functools.partial(far_forward, hb, mb_dev, block_count, sc...  30.2 us
    ppermute x4, starting transfers between devices, from_behind(): return lax.ppermute(x, axis, pairs)  11.8 us
    psum x1, blocking collectives, local(): lax.psum(jnp.stack([jnp.sum(mixed * mixed, axis=(0, 2)), jnp.sum(scaled_g...  10.3 us
    unnamed x39, local copies, waits for them, and re-layouts  7.68 us
  transfers between devices with their start and end apart: 4, of which 0 were waited for; matrix products, arithmetic and copies ran while one was open for 5% of the time, Pallas kernels for 76%

profile of v4, /device:TPU:1, one launch (start us, length us, event | category | flops | bytes accessed | tf_op | source)
XLA Modules:
  0.0 237.0 jit_solution(7060457314362476234)
XLA Ops:
  0.6 4.5 %collective-permute-start = (f32[4,256,128]{2,1,0:T(8,128)}, f32[4,256,128]{2,1,0:T(8,128)}, u32[]{:S(2)}, u32[]{:S(2)}) collective-permute-start(f32[4,256,128]{2,1,0:T(8,128)} %param.11), channel_id=1, source_target_pairs={{0,4},{4,8},{8,12},{12,16},{16,20},{20,24},{24,28},{1,5},{5,9},{9,... | collective-permute-start | bytes 1572872 | tf_op jit(solution)/shard_map/ppermute | solution.py:26
  5.2 1.9 collective-permute-start.1
  7.1 0.8 reshape.106
  7.9 0.5 pad.4.ids_ref
  8.4 30.8 %gather_queries.1 = (f32[8,4,256,128]{3,2,1,0:T(8,128)}, s32[8,1,128]{2,1,0:T(1,128)}) custom-call(f32[4,256,128]{2,1,0:T(8,128)} %x_ref.1, s32[1,128]{1,0:T(1,128)} %pad.4.ids_ref), custom_call_target="tpu_custom_call" | custom-call | bytes 67108864 | tf_op jit(solution)/shard_map/gather_queries/pallas_call | solution.py:148
  39.3 0.7 slice_reduce_fusion
  39.9 0.6 reshape_squeeze.3.ids_ref
  40.6 30.2 %far_forward.1.part_ref = f32[8,4,264,128]{3,2,1,0:T(8,128)} custom-call(s32[256]{0:T(256)} %reshape_squeeze.3.ids_ref, f32[8,4,256,128]{3,2,1,0:T(8,128)} %get-tuple-element.11.q_ref, bf16[4,2048,128]{2,1,0:T(8,128)(2,1)} %k_ref.3, bf16[4,2048,128]{2,1,0:T(8,128)(2,1)} %v_ref.3), custom_call_target="tpu_custom_call" | custom-call | flops 4294967296 | bytes 12582912 | tf_op jit(solution)/shard_map/far_forward/pallas_call | solution.py:375
  70.8 2.2 copy-done
  73.0 24.0 %scatter_out.1 = f32[4,264,128]{2,1,0:T(8,128)S(1)} custom-call(f32[8,4,264,128]{3,2,1,0:T(8,128)S(1)} %copy-done), custom_call_target="tpu_custom_call" | custom-call | bytes 67108864 | tf_op jit(solution)/shard_map/scatter_out/pallas_call | solution.py:215
  97.1 0.0 copy-start.13
  97.8 0.1 pad.8.clone
  97.9 0.2 fusion.7
  98.1 0.0 copy-start.2
  98.1 0.0 collective-permute-done
  98.1 1.1 constant_dynamic-update-slice_fusion.1
  99.2 0.0 copy-done.12
  99.3 0.0 collective-permute-done.1
  99.3 1.1 constant_dynamic-update-slice_fusion.3
  100.5 0.0 copy-start.15
  100.5 0.0 copy-start.14
  100.5 0.0 copy-start.16
  100.5 1.3 fusion.1
  101.8 0.0 copy-start.6
  101.9 0.0 copy-done.14
  101.9 3.1 %multiply_reduce_fusion.3 = (f32[256]{0:T(256)S(1)}, f32[256]{0:T(256)S(1)}, f32[4,256,128]{2,1,0:T(8,128)}, f32[4,256,128]{2,1,0:T(8,128)S(1)}) fusion(f32[4,256,128]{2,1,0:T(8,128)S(1)} %copy-done.14, s32[]{:T(128)} %bitcast.30, s32[4]{0:T(128)S(1)} %multiply_add_fusion.1, f32[4,128]{1,0:T(4,128)S(1)} %copy-done.16, f32[4,256]{1,0:T(4,128)S(1)} %bitcast.32, ...), kind=kOutput, calls=%fused_computation.20 | convolution fusion | flops 407633408 | bytes 5386292 | tf_op jit(solution)/shard_map/hqk,hkd->hqd/dot_general | solution.py:404
  105.0 10.3 %psum.7 = f32[2,256]{1,0:T(2,128)S(1)} all-reduce(f32[2,256]{1,0:T(2,128)S(1)} %pad_maximum_fusion), channel_id=1, replica_groups=mesh['blk'=8,'head'=4] {'head'}, use_global_device_ids=true, to_apply=%region_3.4 | all-reduce | flops 512 | bytes 4096 | tf_op jit(solution)/shard_map/psum | solution.py:421
  115.3 2.6 %multiply_reduce_fusion = (f32[4,256]{1,0:T(4,128)S(1)}, f32[4,256,128]{2,1,0:T(8,128)}, f32[4,256,128]{2,1,0:T(8,128)S(1)}) fusion(f32[4,256]{1,0:T(4,128)S(1)} %bitcast.33, f32[4,264,128]{2,1,0:T(8,128)S(1)} %scatter_out.1, f32[4]{0:T(128)S(1)} %get-tuple-element.21, f32[256]{0:T(256)S(1)} %bitcast.35, f32[4,256,128]{2,1,0:T(8,128)} %get-tuple-element.20, ...), kind=kLoop, calls=%fused_computation.15 | loop fusion | flops 3668992 | bytes 2633764 | tf_op jit(solution)/shard_map/reduce_sum | solution.py:433
  117.9 2.4 fusion.8
  120.3 0.3 multiply_reduce_fusion.1
  120.6 0.0 copy-start.3
  120.6 3.7 %multiply_multiply_fusion = f32[4,256,512]{1,2,0:T(8,128)S(1)} fusion(f32[4,512,128]{2,1,0:T(8,128)} %copy-done.15, f32[4,256]{1,0:T(4,128)S(1)} %multiply_reduce_fusion.1, f32[4,256,128]{2,1,0:T(8,128)} %copy-done.9, f32[4]{0:T(128)S(1)} %get-tuple-element.22, f32[4,256]{1,0:T(4,128)S(1)} %get-tuple-element.27, f32[4,512,256]{2,1,0:T(8,128)} %copy-done.6, ...), kind=kOutput, calls=%fused_computation.1 | convolution fusion | flops 405929984 | bytes 5906448 | tf_op jit(solution)/shard_map/hqd,hkd->hqk/dot_general | solution.py:463
  124.4 0.9 slice.41
  125.2 3.3 %collective-permute-start.3 = (f32[4,256,128]{2,1,0:T(8,128)}, f32[4,256,128]{2,1,0:T(8,128)}, u32[]{:S(2)}, u32[]{:S(2)}) collective-permute-start(f32[4,256,128]{2,1,0:T(8,128)} %slice.41), channel_id=1, source_target_pairs={{4,0},{8,4},{12,8},{16,12},{20,16},{24,20},{28,24},{5,1},{9,5},{13... | collective-permute-start | bytes 1572872 | tf_op jit(solution)/shard_map/ppermute | solution.py:26
  128.5 1.0 fusion.18
  129.6 0.9 copy-done.4
  130.5 0.8 slice.39
  131.4 2.1 collective-permute-start.2
  133.5 0.9 maximum_maximum_fusion.x_ref
  134.4 31.7 %gather_grad.1.g_ref = f32[8,4,264,128]{3,2,1,0:T(8,128)} custom-call(f32[4,264,128]{2,1,0:T(8,128)} %maximum_maximum_fusion.x_ref), custom_call_target="tpu_custom_call" | custom-call | bytes 67108864 | tf_op jit(solution)/shard_map/gather_grad/pallas_call | solution.py:138
  166.1 40.6 %far_backward.1 = (f32[8,4,256,128]{3,2,1,0:T(8,128)}, f32[4,2048,128]{2,1,0:T(8,128)}, f32[4,2048,128]{2,1,0:T(8,128)}) custom-call(s32[256]{0:T(256)} %reshape_squeeze.3.ids_ref, f32[8,4,256,128]{3,2,1,0:T(8,128)} %get-tuple-element.11.q_ref, f32[8,4,264,128]{3,2,1,0:T(8,128)} %gather_grad.1.g_ref, bf16[4,2048,128]{2,1,0:T(8,128)(2,1)} %k_ref.3, ...), custom_call_target="tpu_custom_call" | custom-call | flops 12884901888 | bytes 25165824 | tf_op jit(solution)/shard_map/far_backward/pallas_call | solution.py:443
  206.8 2.2 copy-done.1
  208.9 21.6 %scatter_query_grad.1 = f32[4,256,128]{2,1,0:T(8,128)S(1)} custom-call(f32[8,4,256,128]{3,2,1,0:T(8,128)S(1)} %copy-done.1), custom_call_target="tpu_custom_call" | custom-call | bytes 67108864 | tf_op jit(solution)/shard_map/scatter_query_grad/pallas_call | solution.py:215
  230.6 2.6 %convolution_add_fusion = f32[4,256,128]{2,1,0:T(8,128)} fusion(f32[4,256,512]{1,2,0:T(8,128)S(1)} %multiply_multiply_fusion, f32[4,512,128]{2,1,0:T(8,128)S(1)} %constant_dynamic-update-slice_fusion, f32[4,256,128]{2,1,0:T(8,128)S(1)} %scatter_query_grad.1), kind=kOutput, calls=%fused_computation.4 | convolution fusion | flops 402915328 | bytes 4194304 | tf_op jit(solution)/shard_map/hqk,hkd->hqd/dot_general | solution.py:472
  233.2 0.0 collective-permute-done.3
  233.2 1.9 slice_add_fusion
  235.1 0.0 collective-permute-done.2
  235.1 1.9 slice_add_fusion.1
  (36 shorter events, 0.2 us)
Async XLA Ops:
  0.6 97.5 %collective-permute-start = (f32[4,256,128]{2,1,0:T(8,128)}, f32[4,256,128]{2,1,0:T(8,128)}, u32[]{:S(2)}, u32[]{:S(2)}) collective-permute-start(f32[4,256,128]{2,1,0:T(8,128)} %param.11), channel_id=1, source_target_pairs={{0,4},{4,8},{8,12},{12,16},{16,20},{20,24},{24,28},{1,5},{5,9},{9,... | collective-permute-start | bytes 1572872 | tf_op jit(solution)/shard_map/ppermute | solution.py:26
  5.2 94.2 %collective-permute-start.1 = (f32[4,256,128]{2,1,0:T(8,128)}, f32[4,256,128]{2,1,0:T(8,128)}, u32[]{:S(2)}, u32[]{:S(2)}) collective-permute-start(f32[4,256,128]{2,1,0:T(8,128)} %param.12), channel_id=1, source_target_pairs={{0,4},{4,8},{8,12},{12,16},{16,20},{20,24},{24,28},{1,5},{5,9},{9,... | collective-permute-start | bytes 1572872 | tf_op jit(solution)/shard_map/ppermute | solution.py:26
  70.8 2.2 copy-start
  73.0 24.1 %copy-start.17 = (f32[4]{0:T(128)S(1)}, f32[4]{0:T(128)}, u32[]{:S(2)}) copy-start(f32[4]{0:T(128)} %param.15) | copy-start | bytes 52
  73.0 26.2 %copy-start.12 = (f32[4,256,128]{2,1,0:T(8,128)S(1)}, f32[4,256,128]{2,1,0:T(8,128)}, u32[]{:S(2)}) copy-start(f32[4,256,128]{2,1,0:T(8,128)} %param.11) | copy-start | bytes 1572868
  97.1 3.3 %copy-start.13 = (f32[4,256,128]{2,1,0:T(8,128)S(1)}, f32[4,256,128]{2,1,0:T(8,128)}, u32[]{:S(2)}) copy-start(f32[4,256,128]{2,1,0:T(8,128)} %param.12) | copy-start | bytes 1572868
  98.1 2.4 copy-start.2
  100.5 4.6 %copy-start.15 = (f32[4,512,128]{2,1,0:T(8,128)}, f32[4,512,128]{2,1,0:T(8,128)S(1)}, u32[]{:S(2)}) copy-start(f32[4,512,128]{2,1,0:T(8,128)S(1)} %constant_dynamic-update-slice_fusion.2) | copy-start | bytes 3145732
  100.5 1.4 copy-start.14
  100.5 1.4 copy-start.16
  101.8 3.2 %copy-start.6 = (f32[4,512,256]{2,1,0:T(8,128)}, f32[4,512,256]{2,1,0:T(8,128)S(1)}, u32[]{:S(2)}) copy-start(f32[4,512,256]{2,1,0:T(8,128)S(1)} %get-tuple-element.28) | copy-start | bytes 6291460
  115.3 2.6 %copy-start.7 = (f32[4,512,256]{2,1,0:T(8,128)S(1)}, f32[4,512,256]{2,1,0:T(8,128)}, u32[]{:S(2)}) copy-start(f32[4,512,256]{2,1,0:T(8,128)} %copy-done.6) | copy-start | bytes 6291460
  117.9 2.4 %copy-start.9 = (f32[4,256,128]{2,1,0:T(8,128)}, f32[4,256,128]{2,1,0:T(8,128)S(1)}, u32[]{:S(2)}) copy-start(f32[4,256,128]{2,1,0:T(8,128)S(1)} %get-tuple-element.19) | copy-start | bytes 1572868
  120.6 3.7 %copy-start.10 = (f32[4,512,128]{2,1,0:T(8,128)S(1)}, f32[4,512,128]{2,1,0:T(8,128)}, u32[]{:S(2)}) copy-start(f32[4,512,128]{2,1,0:T(8,128)} %fusion.8) | copy-start | bytes 3145732
  120.6 7.9 %copy-start.3 = (f32[4,256,128]{2,1,0:T(8,128)S(1)}, f32[4,256,128]{2,1,0:T(8,128)}, u32[]{:S(2)}) copy-start(f32[4,256,128]{2,1,0:T(8,128)} %x_ref.1) | copy-start | bytes 1572868
  125.2 8.2 %copy-start.8 = (f32[4,256,128]{2,1,0:T(8,128)S(1)}, f32[4,256,128]{2,1,0:T(8,128)}, u32[]{:S(2)}) copy-start(f32[4,256,128]{2,1,0:T(8,128)} %get-tuple-element.18) | copy-start | bytes 1572868
  125.2 108.0 %collective-permute-start.3 = (f32[4,256,128]{2,1,0:T(8,128)}, f32[4,256,128]{2,1,0:T(8,128)}, u32[]{:S(2)}, u32[]{:S(2)}) collective-permute-start(f32[4,256,128]{2,1,0:T(8,128)} %slice.41), channel_id=1, source_target_pairs={{4,0},{8,4},{12,8},{16,12},{20,16},{24,20},{28,24},{5,1},{9,5},{13... | collective-permute-start | bytes 1572872 | tf_op jit(solution)/shard_map/ppermute | solution.py:26
  129.6 1.0 copy-start.4
  131.4 103.7 %collective-permute-start.2 = (f32[4,256,128]{2,1,0:T(8,128)}, f32[4,256,128]{2,1,0:T(8,128)}, u32[]{:S(2)}, u32[]{:S(2)}) collective-permute-start(f32[4,256,128]{2,1,0:T(8,128)} %slice.39), channel_id=1, source_target_pairs={{4,0},{8,4},{12,8},{16,12},{20,16},{24,20},{28,24},{5,1},{9,5},{13... | collective-permute-start | bytes 1572872 | tf_op jit(solution)/shard_map/ppermute | solution.py:26
  206.8 2.2 copy-start.1
  230.6 2.6 %copy-start.11 = (f32[4,512,128]{2,1,0:T(8,128)S(1)}, f32[4,512,128]{2,1,0:T(8,128)}, u32[]{:S(2)}) copy-start(f32[4,512,128]{2,1,0:T(8,128)} %fusion.8) | copy-start | bytes 3145732
  230.6 4.5 %copy-start.5 = (f32[4,512,128]{2,1,0:T(8,128)S(1)}, f32[4,512,128]{2,1,0:T(8,128)}, u32[]{:S(2)}) copy-start(f32[4,512,128]{2,1,0:T(8,128)} %copy-done.4) | copy-start | bytes 3145732
